TPU v7x, 32 devices: a whole 2x2x4 slice. The times are simulated.
32 devices in a mesh: gx: 4 (over y, x), gy: 8 (over z, core).
Axes of the slice: x: 2, y: 2, z: 4, core: 2. Of those that a mesh axis runs over, the one named last changes fastest.
Arguments:
- state: float32 [8, 8, 64, 1024], P(None, None, 'gx', 'gy'), may hold values from -3 to 3
- residual: float32 [64], replicated, may hold values from -2.5 to 2.5
- shift_rows: int32 [64], P('gx'), may hold values from 0 to 1023
- shear_offset: int32 [1], replicated, may hold values from 0 to 1023
Outputs:
- evolved: float32 [8, 8, 64, 1024], P(None, None, 'gx', 'gy')
Inputs may be any that keep to these rules, and one draw needn't show every extreme that they name: `shift_rows`: each row's whole-cell displacement; it wraps around the 1024 azimuthal cells. `shear_offset`: whole-cell offset of the sheared radial boundary.
All inputs are finite; a program needn't handle non-finite values.
Results may differ from a plain program's by a relative error of at most 0.00002.
Values sent between devices are 32-bit elements; how exact they have to be, the bound alone decides.
A program may use at most 128 MiB of HBM per device.

v0:
```python
import functools

import jax
import jax.numpy as jnp
from jax import lax
from jax.experimental import pallas as pl
from jax.experimental.pallas import tpu as pltpu
from jax.sharding import PartitionSpec as P

time_step = 0.2
viscous = 0.1
resist = 0.1
sound_sq = 1.0
rotation = 0.5
shear_rate = 1.5

MESH = pl.DeviceIdType.MESH
DEPTH = 2


class Copies:
    def __init__(self, send, recv):
        self.send, self.recv, self.made = send, recv, []

    def start(self, source, target, device):
        k = len(self.made)
        copy = pltpu.make_async_remote_copy(
            src_ref=source,
            dst_ref=target,
            send_sem=self.send.at[k],
            recv_sem=self.recv.at[k],
            device_id=device,
            device_id_type=MESH,
        )
        copy.start()
        self.made.append(copy)
        return copy


def copy_count(chips):
    return 8 + sum(10 if 2 * s < chips else 6 for s in range(1, chips // 2 + 1)) + 8 * (chips // 2 + 1)


def gather(state_ref, grid_ref, copies, local_sem, groups, radial):
    rows = state_ref.shape[0]
    chips = groups // 2
    half = rows // 2
    gx, gy = lax.axis_index("gx"), lax.axis_index("gy")
    chip, core = gy // 2, gy % 2

    def at_chip(offset):
        return lax.rem(chip + offset + chips, chips) * 2 + core

    right, left = (gx, at_chip(1)), (gx, at_chip(-1))
    twin = (gx, chip * 2 + (1 - core))
    x_next = (lax.rem(gx + 1, radial), gy)
    x_prev = (lax.rem(gx + radial - 1, radial), gy)

    barrier = pltpu.get_barrier_semaphore()
    for other in (right, left, twin, x_next, x_prev):
        pl.semaphore_signal(barrier, inc=1, device_id=other, device_id_type=MESH)
    pl.semaphore_wait(barrier, 5)

    def piece(block, part):
        return grid_ref.at[block, pl.ds(DEPTH + part * half, half)]

    def low_rows(block):
        return grid_ref.at[block, pl.ds(0, DEPTH)]

    def high_rows(block):
        return grid_ref.at[block, pl.ds(DEPTH + rows, DEPTH)]

    def send_rows(block, part, source):
        if part == 0:
            edge = source.at[pl.ds(0, DEPTH)]
            return block, 0, copies.start(edge, high_rows(block), x_prev)
        edge = source.at[pl.ds(half - DEPTH, DEPTH)]
        return block, 1, copies.start(edge, low_rows(block), x_next)

    to_twin = []

    def pass_rows(sent):
        for block, part, copy in sent:
            copy.wait_recv()
            strip = high_rows(block) if part == 0 else low_rows(block)
            to_twin.append(copies.start(strip, strip, twin))

    own = [state_ref.at[pl.ds(0, half)], state_ref.at[pl.ds(half, half)]]
    keep = pltpu.make_async_copy(state_ref, grid_ref.at[gy, pl.ds(DEPTH, rows)], local_sem)

    flights = []
    order = [(0, 0), (1, 1), (0, 1), (1, 0)] if chips > 2 else [(0, 0), (1, 1)]
    for way, part in order:
        flights.append(
            (way, part, copies.start(own[part], piece(gy, part), right if way == 0 else left))
        )
    sent = [send_rows(gy, part, own[part]) for part in (0, 1)]
    for part in (0, 1):
        to_twin.append(copies.start(own[part], piece(gy, part), twin))
    keep.start()
    pass_rows(sent)
    for step in range(1, chips // 2 + 1):
        later, sent = [], []
        for way, part, copy in flights:
            block = at_chip(-step if way == 0 else step)
            copy.wait_recv()
            ref = piece(block, part)
            if 2 * (step + 1) < chips or (2 * (step + 1) == chips and part == way):
                later.append((way, part, copies.start(ref, ref, right if way == 0 else left)))
            to_twin.append(copies.start(ref, ref, twin))
            sent.append(send_rows(block, part, ref))
        pass_rows(sent)
        flights = later
    keep.wait()
    for copy in to_twin:
        copy.wait_recv()
    for copy in copies.made:
        copy.wait_send()


def row_sweep(load, first_row, last_row, drift_of, emit):
    def y_ahead(a):
        return pltpu.roll(a, a.shape[1] - 1, 1)

    def y_behind(a):
        return pltpu.roll(a, 1, 1)

    def z_ahead(a):
        return pltpu.roll(a, a.shape[0] - 1, 0)

    def z_behind(a):
        return pltpu.roll(a, 1, 0)

    def cells(by, bz):
        return 0.5 * (by + y_ahead(by)), 0.5 * (bz + z_ahead(bz))

    def radial_edges(prev, cur, prev_drift, cur_drift):
        sum_x = prev[1] + cur[1]
        sum_w = (prev[2] + prev_drift) + (cur[2] + cur_drift)
        sum_z = prev[3] + cur[3]
        bx, by, bz = cur[5], cur[6], cur[7]
        bx_y, bx_z = y_behind(bx), z_behind(bx)
        emf_z = 0.125 * (
            (sum_w + y_behind(sum_w)) * (bx + bx_y) - (sum_x + y_behind(sum_x)) * (by + prev[6])
        ) + resist * ((by - prev[6]) - (bx - bx_y))
        emf_y = 0.125 * (
            (sum_x + z_behind(sum_x)) * (bz + prev[7]) - (sum_z + z_behind(sum_z)) * (bx + bx_z)
        ) + resist * ((bx - bx_z) - (bz - prev[7]))
        return emf_z, emf_y

    start_prev, start_cur = load(first_row - 1), load(first_row)
    carry = (
        *cells(start_prev[6], start_prev[7]),
        *cells(start_cur[6], start_cur[7]),
        *radial_edges(start_prev, start_cur, drift_of(first_row - 1), drift_of(first_row)),
    )

    def one(row, carry):
        cy_prev, cz_prev, cy, cz, emf_z, emf_y = carry
        prev, cur, nxt = load(row - 1), load(row), load(row + 1)
        drift = drift_of(row)
        log_rho, vx, vy, vz, ent, bx, by, bz = cur
        w = vy + drift
        cy_next, cz_next = cells(nxt[6], nxt[7])
        emf_z_next, emf_y_next = radial_edges(cur, nxt, drift, drift_of(row + 1))

        half_x, half_w, half_z = 0.5 * vx, 0.5 * w, 0.5 * vz
        diffs, advs = [], []
        for f in range(5):
            a = cur[f]
            ya, yb, za, zb = y_ahead(a), y_behind(a), z_ahead(a), z_behind(a)
            dx, dy, dz = nxt[f] - prev[f], ya - yb, za - zb
            lap = ((nxt[f] + prev[f]) + (ya + yb) + (za + zb)) - 6.0 * a
            diffs.append((dx, dy, dz))
            advs.append(viscous * lap - (half_x * dx + half_w * dy + half_z * dz))

        sum_bx = bx + nxt[5]
        cx = 0.5 * sum_bx
        cur_x = 0.5 * ((y_ahead(cz) - y_behind(cz)) - (z_ahead(cy) - z_behind(cy)))
        cur_y = 0.5 * ((z_ahead(cx) - z_behind(cx)) - (cz_next - cz_prev))
        cur_z = 0.5 * ((cy_next - cy_prev) - (y_ahead(cx) - y_behind(cx)))
        inverse = jnp.exp(-log_rho)
        force_x = inverse * (cur_y * cz - cur_z * cy)
        force_y = inverse * (cur_z * cx - cur_x * cz)
        force_z = inverse * (cur_x * cy - cur_y * cx)

        pairs = [diffs[0][d] + diffs[4][d] for d in range(3)]
        rates = [
            advs[0] - 0.5 * (diffs[1][0] + diffs[2][1] + diffs[3][2]),
            advs[1] - (0.5 * sound_sq) * pairs[0] + force_x + (2.0 * rotation) * vy,
            advs[2] - (0.5 * sound_sq) * pairs[1] + force_y - ((2.0 - shear_rate) * rotation) * vx,
            advs[3] - (0.5 * sound_sq) * pairs[2] + force_z,
            advs[4] + resist * inverse * (cur_x * cur_x + cur_y * cur_y + cur_z * cur_z),
        ]

        w_y, z_y = w + y_behind(w), vz + y_behind(vz)
        bz_y, by_z = y_behind(bz), z_behind(by)
        emf_x = 0.125 * (
            (z_y + z_behind(z_y)) * (by + by_z) - (w_y + z_behind(w_y)) * (bz + bz_y)
        ) + resist * ((bz - bz_y) - (by - by_z))
        stretch = 0.25 * (sum_bx + y_behind(sum_bx))
        rates.append((z_ahead(emf_y) - emf_y) - (y_ahead(emf_z) - emf_z))
        rates.append(
            (emf_z_next - emf_z) - (z_ahead(emf_x) - emf_x) - (shear_rate * rotation) * stretch
        )
        rates.append((y_ahead(emf_x) - emf_x) - (emf_y_next - emf_y))
        emit(row, cur, rates)
        return cy, cz, cy_next, cz_next, emf_z_next, emf_y_next

    if last_row - first_row < 3:
        for row in range(first_row, last_row + 1):
            carry = one(row, carry)
        return
    lax.fori_loop(first_row, last_row + 1, one, carry, unroll=2)


def step_kernel(
    groups, radial, state_ref, table_ref, drift_ref, out_ref,
    grid_ref, moved_ref, first_ref, send, recv, local_sem,
):
    rows, fields, _, cols = state_ref.shape
    gather(state_ref, grid_ref, Copies(send, recv), local_sem, groups, radial)

    lane = lax.broadcasted_iota(jnp.int32, state_ref.shape[2:], 1)

    def turn(row, _):
        amount = table_ref[4, row]
        inside = lane < cols - amount
        low_side = lane < cols // 2
        blocks = [table_ref[k, row] for k in range(4)]
        for f in range(fields):
            before, here, after, beyond = [
                pltpu.roll(grid_ref[b, row, f], cols - amount, 1) for b in blocks
            ]
            moved_ref[row, f, :, :cols] = jnp.where(inside, here, after)
            moved_ref[row, f, :, cols:] = jnp.where(
                low_side, jnp.where(inside, after, beyond), jnp.where(inside, before, here)
            )
        return 0

    lax.fori_loop(0, rows + 2 * DEPTH, turn, 0)

    def drift_of(row):
        return drift_ref[row]

    def emit_first(row, cur, rates):
        for f in range(fields):
            first_ref[row, f] = cur[f] + time_step * rates[f]

    def emit_out(row, cur, rates):
        for f in range(fields):
            second = cur[f][:, :cols] + time_step * rates[f][:, :cols]
            out_ref[row - DEPTH, f] = 0.5 * (moved_ref[row, f, :, :cols] + second)

    def load_from(ref):
        return lambda row: [ref[row, f] for f in range(fields)]

    row_sweep(load_from(moved_ref), 1, rows + 2, drift_of, emit_first)
    row_sweep(load_from(first_ref), 2, rows + 1, drift_of, emit_out)


def gathered(state, residual, shift_rows, shear_offset):
    fields, vertical, rows, cols = state.shape
    groups, radial = lax.axis_size("gy"), lax.axis_size("gx")
    gx, gy = lax.axis_index("gx"), lax.axis_index("gy")
    cells_y = cols * groups
    wide = rows + 2 * DEPTH

    up = [(i, (i + 1) % radial) for i in range(radial)]
    down = [(target, source) for source, target in up]
    low = lax.ppermute(shift_rows[-DEPTH:], "gx", up)
    high = lax.ppermute(shift_rows[:DEPTH], "gx", down)
    offset = shear_offset[0]
    low = low - jnp.where(gx == 0, offset, 0)
    high = high + jnp.where(gx == radial - 1, offset, 0)
    amounts = jnp.concatenate([low, shift_rows, high])
    origin = (cols * gy - amounts) % cells_y
    block, part = origin // cols, origin % cols
    table = jnp.stack(
        [(block + groups - 1) % groups, block, (block + 1) % groups, (block + 2) % groups, part]
    )
    padded = jnp.concatenate([residual[-DEPTH:], residual, residual[:DEPTH]])
    drift = lax.dynamic_slice_in_dim(padded, gx * rows, wide)

    count = copy_count(groups // 2)
    out = pl.pallas_call(
        functools.partial(step_kernel, groups, radial),
        out_shape=jax.ShapeDtypeStruct((rows, fields, vertical, cols), jnp.float32),
        in_specs=[
            pl.BlockSpec(memory_space=pltpu.VMEM),
            pl.BlockSpec(memory_space=pltpu.SMEM),
            pl.BlockSpec(memory_space=pltpu.SMEM),
        ],
        out_specs=pl.BlockSpec(memory_space=pltpu.VMEM),
        scratch_shapes=[
            pltpu.VMEM((groups, wide, fields, vertical, cols), jnp.float32),
            pltpu.VMEM((wide, fields, vertical, 2 * cols), jnp.float32),
            pltpu.VMEM((wide, fields, vertical, 2 * cols), jnp.float32),
            pltpu.SemaphoreType.DMA((count,)),
            pltpu.SemaphoreType.DMA((count,)),
            pltpu.SemaphoreType.DMA,
        ],
        compiler_params=pltpu.CompilerParams(collective_id=0, has_side_effects=True),
    )(jnp.transpose(state, (2, 0, 1, 3)), table, drift)
    return jnp.transpose(out, (1, 2, 0, 3))


def spread_kernel(
    groups, radial, state_ref, shift_hbm, offset_hbm, residual_hbm, out_ref,
    shift_ref, offset_ref, residual_ref, taken_a, taken_b, turned_ref, low_ref, high_ref, back_ref, moved_ref, first_ref,
    send, recv, local_sems,
):
    fields, vertical, rows, cols = state_ref.shape
    half = rows // 2
    gx, gy = lax.axis_index("gx"), lax.axis_index("gy")
    copies = Copies(send, recv)
    x_next = (lax.rem(gx + 1, radial), gy)
    x_prev = (lax.rem(gx + radial - 1, radial), gy)
    others = [(gx, lax.rem(gy + k, groups)) for k in range(1, groups)]

    small = [
        pltpu.make_async_copy(source, target, local_sems.at[5 + k])
        for k, (source, target) in enumerate(
            ((shift_hbm, shift_ref), (offset_hbm, offset_ref), (residual_hbm, residual_ref))
        )
    ]
    for copy in small:
        copy.start()
    barrier = pltpu.get_barrier_semaphore()
    for other in (*others, x_prev, x_next):
        pl.semaphore_signal(barrier, inc=1, device_id=other, device_id_type=MESH)
    pl.semaphore_wait(barrier, groups + 1)

    def part_rows(part):
        return pl.ds(part * half, half)

    taken = (taken_a, taken_b)
    out_flights, keep = [], []
    for part in (0, 1):
        out_flights.append([
            copies.start(
                state_ref.at[other[1], :, part_rows(part)],
                taken[part].at[gy],
                other,
            )
            for other in others
        ])
        keep.append(
            pltpu.make_async_copy(
                state_ref.at[gy, :, part_rows(part)], taken[part].at[gy], local_sems.at[part]
            )
        )
        keep[part].start()

    lane = lax.broadcasted_iota(jnp.int32, (vertical, cols), 1)

    def displace(block_of, amount, place, slot, packed):
        whole, part = amount // cols, amount % cols
        rolled = [
            pltpu.roll(block_of(lax.rem(k - whole + groups, groups)), part, 1)
            for k in range(groups)
        ]
        row = [jnp.where(lane < part, rolled[d - 1], rolled[d]) for d in range(groups)]
        mine = (lane >= 4 * place) & (lane < 4 * place + 4)
        result = []
        for d in range(groups):
            turned_ref[d, slot] = row[d]
            edges = jnp.where(lane < cols // 2, row[(d + 1) % groups], row[d - 1])
            result.append(jnp.where(mine, pltpu.roll(edges, 4 * place + 2, 1), packed[d]))
        return result

    empty = [jnp.zeros((vertical, cols), jnp.float32)] * groups

    def store_packed(slot, packed):
        for d in range(groups):
            turned_ref[d, slot] = packed[d]

    back_flights, kept = [], []

    def send_back(index, first_slot, count):
        span = pl.ds(first_slot, count)
        back_flights.append([
            copies.start(turned_ref.at[other[1], span], back_ref.at[gy, span], other)
            for other in others
        ])
        stay = pltpu.make_async_copy(
            turned_ref.at[gy, span], back_ref.at[gy, span], local_sems.at[2 + index]
        )
        stay.start()
        kept.append(stay)

    ghosts, packed = [], empty
    for copy in small:
        copy.wait()
    for part in (0, 1):
        for copy in out_flights[part]:
            copy.wait_recv()
        keep[part].wait()
        for place in range(half):
            row = part * half + place
            packed = displace(
                lambda b: taken[part][b, :, place, :], shift_ref[row], row, row, packed
            )
        if part == 0:
            ghosts.append(copies.start(turned_ref.at[:, pl.ds(0, DEPTH)], high_ref, x_prev))
        else:
            store_packed(rows, packed)
            edge = pl.ds(rows - DEPTH, DEPTH)
            ghosts.append(copies.start(turned_ref.at[:, edge], low_ref, x_next))
        send_back(part, part * half, half + part)

    for copy in ghosts:
        copy.wait_recv()
    cells_y = cols * groups
    offset = offset_ref[0]
    turn_low = jnp.where(gx == 0, lax.rem(cells_y - offset, cells_y), 0)
    turn_high = jnp.where(gx == radial - 1, offset, 0)
    packed = empty
    for place in range(2 * DEPTH):
        ref, amount = (low_ref, turn_low) if place < DEPTH else (high_ref, turn_high)
        packed = displace(
            lambda b: ref[b, place % DEPTH], amount, place, rows + 1 + place, packed
        )
    store_packed(rows + 1 + 2 * DEPTH, packed)
    send_back(2, rows + 1, 2 * DEPTH + 1)

    def arrive(indices, first_slot, count, row_of):
        for index in indices:
            for copy in back_flights[index]:
                copy.wait_recv()
            kept[index].wait()
        for f in range(fields):
            packed = back_ref[f, first_slot + count]
            for place in range(count):
                moved_ref[row_of(place), f, :, :cols] = back_ref[f, first_slot + place]
                moved_ref[row_of(place), f, :, cols:] = pltpu.roll(
                    packed, (cols - 2 - 4 * place) % cols, 1
                )

    start = gx * rows - DEPTH + residual_ref.shape[0]

    def drift_of(row):
        return residual_ref[lax.rem(start + row, residual_ref.shape[0])]

    def emit_first(row, cur, rates):
        for f in range(fields):
            first_ref[row, f] = cur[f] + time_step * rates[f]

    def emit_out(row, cur, rates):
        for f in range(fields):
            second = cur[f][:, :cols] + time_step * rates[f][:, :cols]
            out_ref[f, :, row - DEPTH, :] = 0.5 * (moved_ref[row, f, :, :cols] + second)

    def load_from(ref):
        return lambda row: [ref[row, f] for f in range(fields)]

    def stage_one(low, high):
        row_sweep(load_from(moved_ref), low, high, drift_of, emit_first)

    def stage_two(low, high):
        row_sweep(load_from(first_ref), low, high, drift_of, emit_out)

    arrive((0, 1), 0, rows, lambda place: DEPTH + place)
    stage_one(3, rows)
    stage_two(4, rows - 1)
    arrive(
        (2,), rows + 1, 2 * DEPTH, lambda place: place if place < DEPTH else rows + place
    )
    stage_one(1, 2)
    stage_one(rows + 1, rows + 2)
    stage_two(2, 3)
    stage_two(rows, rows + 1)
    for copy in copies.made:
        copy.wait_send()


def spread(state, residual, shift_rows, shear_offset):
    fields, vertical, rows, cols = state.shape
    groups, radial = lax.axis_size("gy"), lax.axis_size("gx")
    wide = rows + 2 * DEPTH
    slots = rows + 2 * DEPTH + 2
    count = 5 * (groups - 1) + 2
    anywhere = pl.BlockSpec(memory_space=pl.ANY)
    vmem = pl.BlockSpec(memory_space=pltpu.VMEM)
    out = pl.pallas_call(
        functools.partial(spread_kernel, groups, radial),
        out_shape=jax.ShapeDtypeStruct(state.shape, jnp.float32),
        in_specs=[anywhere] * 4,
        out_specs=vmem,
        scratch_shapes=[
            pltpu.SMEM(shift_rows.shape, jnp.int32),
            pltpu.SMEM(shear_offset.shape, jnp.int32),
            pltpu.SMEM(residual.shape, jnp.float32),
            pltpu.VMEM((groups, vertical, rows // 2, cols), jnp.float32),
            pltpu.VMEM((groups, vertical, rows // 2, cols), jnp.float32),
            pltpu.VMEM((groups, slots, vertical, cols), jnp.float32),
            pltpu.VMEM((groups, DEPTH, vertical, cols), jnp.float32),
            pltpu.VMEM((groups, DEPTH, vertical, cols), jnp.float32),
            pltpu.VMEM((fields, slots, vertical, cols), jnp.float32),
            pltpu.VMEM((wide, fields, vertical, 2 * cols), jnp.float32),
            pltpu.VMEM((wide, fields, vertical, 2 * cols), jnp.float32),
            pltpu.SemaphoreType.DMA((count,)),
            pltpu.SemaphoreType.DMA((count,)),
            pltpu.SemaphoreType.DMA((8,)),
        ],
        compiler_params=pltpu.CompilerParams(collective_id=1, has_side_effects=True),
    )(state, shift_rows, shear_offset, residual)
    return out


def local(state, residual, shift_rows, shear_offset):
    if lax.axis_size("gy") == state.shape[0] and state.shape[2] % 16 == 0:
        return spread(state, residual, shift_rows, shear_offset)
    return gathered(state, residual, shift_rows, shear_offset)


def solution(mesh):
    return jax.shard_map(
        local,
        mesh=mesh,
        in_specs=(P(None, None, "gx", "gy"), P(), P("gx"), P()),
        out_specs=P(None, None, "gx", "gy"),
        check_vma=False,
    )
```

profile of v0, /device:TPU:0, one launch (start us, length us, event | category | flops | bytes accessed | tf_op | source)
XLA Modules:
  0.0 38.4 jit_solution(15215318327767883345)
XLA Ops:
  0.7 35.9 %shard_map.46 = f32[8,8,16,128]{3,2,1,0:T(8,128)} custom-call(f32[8,8,16,128]{3,2,1,0:T(8,128)} %state_ref.1, s32[16]{0:T(128)} %shift_hbm.1, s32[1]{0:T(128)S(6)} %copy.6.offset_hbm, f32[64]{0:T(128)} %residual_hbm.1), custom_call_target="tpu_custom_call" | custom-call | tf_op jit(solution)/shard_map/pallas_call | solution.py:485
  36.5 1.9 %copy.7 = f32[8,8,16,128]{3,2,1,0:T(8,128)} copy(f32[8,8,16,128]{3,2,1,0:T(8,128)} %shard_map.46) | data formatting | bytes 1048576
where the time goes:
time: 38.8 us; the launch traced here: 38.4 us
  Pallas kernels  35.9 us (93%)
  local copies, waits for them, and re-layouts  1.87 us (5%)
  between operations  0.66 us (2%)
    pallas_call x1, Pallas kernels, spread(): pl.pallas_call(functools.partial(spread_kernel, groups, radial), out_shap...  35.9 us
    unnamed x1, local copies, waits for them, and re-layouts  1.87 us

commit v1 on v0

--- a/solution.py
+++ b/solution.py
@@ -449,7 +449,7 @@
     def emit_out(row, cur, rates):
         for f in range(fields):
             second = cur[f][:, :cols] + time_step * rates[f][:, :cols]
-            out_ref[f, :, row - DEPTH, :] = 0.5 * (moved_ref[row, f, :, :cols] + second)
+            out_ref[f, :, row - DEPTH, :] = moved_ref[row, f, :, :cols] + second
 
     def load_from(ref):
         return lambda row: [ref[row, f] for f in range(fields)]
@@ -484,7 +484,7 @@
     vmem = pl.BlockSpec(memory_space=pltpu.VMEM)
     out = pl.pallas_call(
         functools.partial(spread_kernel, groups, radial),
-        out_shape=jax.ShapeDtypeStruct(state.shape, jnp.float32),
+        out_shape=pltpu.VMEM(state.shape, jnp.float32),
         in_specs=[anywhere] * 4,
         out_specs=vmem,
         scratch_shapes=[
@@ -505,7 +505,7 @@
         ],
         compiler_params=pltpu.CompilerParams(collective_id=1, has_side_effects=True),
     )(state, shift_rows, shear_offset, residual)
-    return out
+    return 0.5 * out
 
 
 def local(state, residual, shift_rows, shear_offset):

time: 38.8 us -> 37 us (0.954)
  local copies, waits for them, and re-layouts: 1.87 us -> 0 us
  other arithmetic: 0 us -> 0.84 us
  Pallas kernels: 35.9 us -> 35.1 us
    unnamed x1 -> x0, local copies, waits for them, and re-layouts: 1.87 us -> none
    mul x0 -> x1, other arithmetic: none -> 0.84 us  [spread(): return 0.5 * out]
    pallas_call x1, Pallas kernels: 35.9 us -> 35.1 us  [spread(): pl.pallas_call(functools.partial(spread_kernel, groups, radial), out_shap...]
where the time goes in v1:
time: 37 us; the launch traced here: 36.6 us
  Pallas kernels  35.1 us (95%)
  other arithmetic  0.84 us (2%)
  between operations  0.66 us (2%)
    pallas_call x1, Pallas kernels, spread(): pl.pallas_call(functools.partial(spread_kernel, groups, radial), out_shap...  35.1 us
    mul x1, other arithmetic, spread(): return 0.5 * out  0.84 us

profile of v1, /device:TPU:0, one launch (start us, length us, event | category | flops | bytes accessed | tf_op | source)
XLA Modules:
  0.0 36.6 jit_solution(12085177353229513209)
XLA Ops:
  0.7 35.1 %shard_map.46 = f32[8,8,16,128]{3,2,1,0:T(8,128)S(1)} custom-call(f32[8,8,16,128]{3,2,1,0:T(8,128)} %state_ref.1, s32[16]{0:T(128)} %shift_hbm.1, s32[1]{0:T(128)S(6)} %copy.5.offset_hbm, f32[64]{0:T(128)} %residual_hbm.1), custom_call_target="tpu_custom_call" | custom-call | tf_op jit(solution)/shard_map/pallas_call | solution.py:485
  35.7 0.8 %broadcast_multiply_fusion = f32[8,8,16,128]{3,2,1,0:T(8,128)} fusion(f32[8,8,16,128]{3,2,1,0:T(8,128)S(1)} %shard_map.46), kind=kLoop, calls=%fused_computation | loop fusion | flops 131072 | bytes 1048576 | tf_op jit(solution)/shard_map/mul | solution.py:508

commit v2 on v1

--- a/solution.py
+++ b/solution.py
@@ -307,52 +307,57 @@
 
 def spread_kernel(
     groups, radial, state_ref, shift_hbm, offset_hbm, residual_hbm, out_ref,
-    shift_ref, offset_ref, residual_ref, taken_a, taken_b, turned_ref, low_ref, high_ref, back_ref, moved_ref, first_ref,
-    send, recv, local_sems,
+    shift_ref, offset_ref, residual_ref, taken_0, taken_1, taken_2, taken_3, turned_ref, edge_ref,
+    shear_ref, moved_ref, own_edges, low_edges, high_edges, first_ref, send, recv, local_sems,
 ):
     fields, vertical, rows, cols = state_ref.shape
-    half = rows // 2
+    quarter = rows // 4
+    taken = (taken_0, taken_1, taken_2, taken_3)
+    cells_y = cols * groups
     gx, gy = lax.axis_index("gx"), lax.axis_index("gy")
     copies = Copies(send, recv)
     x_next = (lax.rem(gx + 1, radial), gy)
     x_prev = (lax.rem(gx + radial - 1, radial), gy)
     others = [(gx, lax.rem(gy + k, groups)) for k in range(1, groups)]
+    first_x, last_x = gx == 0, gx == radial - 1
+    stays = []
+
+    def stay(source, target):
+        copy = pltpu.make_async_copy(source, target, local_sems.at[len(stays)])
+        copy.start()
+        stays.append(copy)
+        return copy
 
     small = [
-        pltpu.make_async_copy(source, target, local_sems.at[5 + k])
-        for k, (source, target) in enumerate(
-            ((shift_hbm, shift_ref), (offset_hbm, offset_ref), (residual_hbm, residual_ref))
+        stay(source, target)
+        for source, target in (
+            (shift_hbm, shift_ref), (offset_hbm, offset_ref), (residual_hbm, residual_ref)
         )
     ]
-    for copy in small:
-        copy.start()
     barrier = pltpu.get_barrier_semaphore()
     for other in (*others, x_prev, x_next):
         pl.semaphore_signal(barrier, inc=1, device_id=other, device_id_type=MESH)
     pl.semaphore_wait(barrier, groups + 1)
 
-    def part_rows(part):
-        return pl.ds(part * half, half)
-
-    taken = (taken_a, taken_b)
-    out_flights, keep = [], []
-    for part in (0, 1):
-        out_flights.append([
+    def quarter_rows(q):
+        return pl.ds(q * quarter, quarter)
+
+    out_flights = {}
+    for q in (0, 3, 1, 2):
+        out_flights[q] = [
             copies.start(
-                state_ref.at[other[1], :, part_rows(part)],
-                taken[part].at[gy],
-                other,
+                state_ref.at[other[1], :, quarter_rows(q)], taken[q].at[gy], other
             )
             for other in others
-        ])
-        keep.append(
-            pltpu.make_async_copy(
-                state_ref.at[gy, :, part_rows(part)], taken[part].at[gy], local_sems.at[part]
-            )
-        )
-        keep[part].start()
+        ]
+        out_flights[q].append(stay(state_ref.at[gy, :, quarter_rows(q)], taken[q].at[gy]))
+
+    def wait_all(flights):
+        for copy in flights:
+            copy.wait() if any(copy is s for s in stays) else copy.wait_recv()
 
     lane = lax.broadcasted_iota(jnp.int32, (vertical, cols), 1)
+    empty = [jnp.zeros((vertical, cols), jnp.float32)] * groups
 
     def displace(block_of, amount, place, slot, packed):
         whole, part = amount // cols, amount % cols
@@ -369,72 +374,124 @@
             result.append(jnp.where(mine, pltpu.roll(edges, 4 * place + 2, 1), packed[d]))
         return result
 
-    empty = [jnp.zeros((vertical, cols), jnp.float32)] * groups
-
-    def store_packed(slot, packed):
-        for d in range(groups):
-            turned_ref[d, slot] = packed[d]
-
-    back_flights, kept = [], []
-
-    def send_back(index, first_slot, count):
-        span = pl.ds(first_slot, count)
-        back_flights.append([
-            copies.start(turned_ref.at[other[1], span], back_ref.at[gy, span], other)
+    def displace_quarter(q, packed):
+        wait_all(out_flights[q])
+        for place in range(quarter):
+            row = q * quarter + place
+            packed = displace(
+                lambda b: taken[q][b, :, place, :], shift_ref[row], row, row, packed
+            )
+        return packed
+
+    def main_lanes(block, first_row, count):
+        return moved_ref.at[block, pl.ds(first_row, count), :, pl.ds(0, cols)]
+
+    def send_back(slot, first_row, count):
+        span = pl.ds(slot, count)
+        flights = [
+            copies.start(turned_ref.at[other[1], span], main_lanes(gy, first_row, count), other)
             for other in others
-        ])
-        stay = pltpu.make_async_copy(
-            turned_ref.at[gy, span], back_ref.at[gy, span], local_sems.at[2 + index]
-        )
-        stay.start()
-        kept.append(stay)
-
-    ghosts, packed = [], empty
+        ]
+        flights.append(stay(turned_ref.at[gy, span], main_lanes(gy, first_row, count)))
+        return flights
+
+    def make(source, target, device):
+        k = len(copies.made)
+        copy = pltpu.make_async_remote_copy(
+            src_ref=source,
+            dst_ref=target,
+            send_sem=send.at[k],
+            recv_sem=recv.at[k],
+            device_id=device,
+            device_id_type=MESH,
+        )
+        copies.made.append(copy)
+        optional.append(copy)
+        return copy
+
+    optional = []
     for copy in small:
         copy.wait()
-    for part in (0, 1):
-        for copy in out_flights[part]:
-            copy.wait_recv()
-        keep[part].wait()
-        for place in range(half):
-            row = part * half + place
-            packed = displace(
-                lambda b: taken[part][b, :, place, :], shift_ref[row], row, row, packed
+    packed = displace_quarter(0, empty)
+    back = {0: send_back(0, DEPTH, quarter)}
+    packed = displace_quarter(3, packed)
+    to_last = make(turned_ref.at[:, pl.ds(0, DEPTH)], shear_ref, x_prev)
+    to_first = make(turned_ref.at[:, pl.ds(rows - DEPTH, DEPTH)], shear_ref, x_next)
+    pl.when(first_x)(to_last.start)
+    pl.when(last_x)(to_first.start)
+    back[3] = send_back(3 * quarter, DEPTH + 3 * quarter, quarter)
+
+    def sheared(first_row, flight, amount):
+        flight.wait_recv()
+        edges = empty
+        for place in range(DEPTH):
+            edges = displace(
+                lambda b: shear_ref[b, place], amount, rows + place, rows + place, edges
             )
-        if part == 0:
-            ghosts.append(copies.start(turned_ref.at[:, pl.ds(0, DEPTH)], high_ref, x_prev))
-        else:
-            store_packed(rows, packed)
-            edge = pl.ds(rows - DEPTH, DEPTH)
-            ghosts.append(copies.start(turned_ref.at[:, edge], low_ref, x_next))
-        send_back(part, part * half, half + part)
-
-    for copy in ghosts:
-        copy.wait_recv()
-    cells_y = cols * groups
+        for d in range(groups):
+            edge_ref[d] = edges[d]
+        for copy in shear_back[first_row]:
+            copy.start()
+
+    span = pl.ds(rows, DEPTH)
+    low_row, high_row = 0, DEPTH + rows
+    shear_back = {}
+    for first_row in (low_row, high_row):
+        shear_back[first_row] = [
+            make(turned_ref.at[other[1], span], main_lanes(gy, first_row, DEPTH), other)
+            for other in others
+        ]
+        copy = pltpu.make_async_copy(
+            turned_ref.at[gy, span], main_lanes(gy, first_row, DEPTH), local_sems.at[len(stays)]
+        )
+        stays.append(copy)
+        shear_back[first_row].append(copy)
     offset = offset_ref[0]
-    turn_low = jnp.where(gx == 0, lax.rem(cells_y - offset, cells_y), 0)
-    turn_high = jnp.where(gx == radial - 1, offset, 0)
-    packed = empty
-    for place in range(2 * DEPTH):
-        ref, amount = (low_ref, turn_low) if place < DEPTH else (high_ref, turn_high)
-        packed = displace(
-            lambda b: ref[b, place % DEPTH], amount, place, rows + 1 + place, packed
-        )
-    store_packed(rows + 1 + 2 * DEPTH, packed)
-    send_back(2, rows + 1, 2 * DEPTH + 1)
-
-    def arrive(indices, first_slot, count, row_of):
-        for index in indices:
-            for copy in back_flights[index]:
-                copy.wait_recv()
-            kept[index].wait()
+    for d in range(groups):
+        edge_ref[d] = empty[0]
+
+    @pl.when(first_x)
+    def _():
+        sheared(low_row, to_first, lax.rem(cells_y - offset, cells_y))
+
+    @pl.when(last_x)
+    def _():
+        sheared(high_row, to_last, offset)
+
+    packed = displace_quarter(1, packed)
+    packed = displace_quarter(2, packed)
+    for d in range(groups):
+        edge_ref[d] = jnp.where(lane < 4 * rows, packed[d], edge_ref[d])
+    edge_flights = [
+        copies.start(edge_ref.at[other[1]], own_edges.at[gy], other) for other in others
+    ]
+    edge_flights.append(stay(edge_ref.at[gy], own_edges.at[gy]))
+    for q in (1, 2):
+        back[q] = send_back(q * quarter, DEPTH + q * quarter, quarter)
+
+    for q in (0, 3):
+        wait_all(back[q])
+    rows_down = make(
+        main_lanes(slice(None), DEPTH, DEPTH), main_lanes(slice(None), high_row, DEPTH), x_prev
+    )
+    rows_up = make(
+        main_lanes(slice(None), rows, DEPTH), main_lanes(slice(None), low_row, DEPTH), x_next
+    )
+    edges_down = make(own_edges, high_edges, x_prev)
+    edges_up = make(own_edges, low_edges, x_next)
+    not_first, not_last = gx > 0, gx < radial - 1
+    pl.when(not_first)(rows_down.start)
+    pl.when(not_last)(rows_up.start)
+    wait_all(edge_flights)
+    pl.when(not_first)(edges_down.start)
+    pl.when(not_last)(edges_up.start)
+
+    def unpack(edges_ref, first_place, first_row, count):
         for f in range(fields):
-            packed = back_ref[f, first_slot + count]
-            for place in range(count):
-                moved_ref[row_of(place), f, :, :cols] = back_ref[f, first_slot + place]
-                moved_ref[row_of(place), f, :, cols:] = pltpu.roll(
-                    packed, (cols - 2 - 4 * place) % cols, 1
+            packed = edges_ref[f]
+            for k in range(count):
+                moved_ref[f, first_row + k, :, cols:] = pltpu.roll(
+                    packed, (cols - 2 - 4 * (first_place + k)) % cols, 1
                 )
 
     start = gx * rows - DEPTH + residual_ref.shape[0]
@@ -449,39 +506,92 @@
     def emit_out(row, cur, rates):
         for f in range(fields):
             second = cur[f][:, :cols] + time_step * rates[f][:, :cols]
-            out_ref[f, :, row - DEPTH, :] = moved_ref[row, f, :, :cols] + second
-
-    def load_from(ref):
-        return lambda row: [ref[row, f] for f in range(fields)]
+            out_ref[f, :, row - DEPTH, :] = moved_ref[f, row, :, :cols] + second
 
     def stage_one(low, high):
-        row_sweep(load_from(moved_ref), low, high, drift_of, emit_first)
+        row_sweep(
+            lambda row: [moved_ref[f, row] for f in range(fields)],
+            DEPTH + low, DEPTH + high, drift_of, emit_first,
+        )
 
     def stage_two(low, high):
-        row_sweep(load_from(first_ref), low, high, drift_of, emit_out)
-
-    arrive((0, 1), 0, rows, lambda place: DEPTH + place)
-    stage_one(3, rows)
-    stage_two(4, rows - 1)
-    arrive(
-        (2,), rows + 1, 2 * DEPTH, lambda place: place if place < DEPTH else rows + place
-    )
-    stage_one(1, 2)
-    stage_one(rows + 1, rows + 2)
-    stage_two(2, 3)
-    stage_two(rows, rows + 1)
+        row_sweep(
+            lambda row: [first_ref[row, f] for f in range(fields)],
+            DEPTH + low, DEPTH + high, drift_of, emit_out,
+        )
+
+    unpack(own_edges, 0, DEPTH, rows)
+    stage_one(1, quarter - 2)
+    stage_one(3 * quarter + 1, rows - 2)
+
+    @pl.when(first_x)
+    def _():
+        wait_all(shear_back[low_row])
+        unpack(own_edges, rows, low_row, DEPTH)
+
+    @pl.when(not_first)
+    def _():
+        rows_up.wait_recv()
+        edges_up.wait_recv()
+        unpack(low_edges, rows - DEPTH, low_row, DEPTH)
+
+    @pl.when(last_x)
+    def _():
+        wait_all(shear_back[high_row])
+        unpack(own_edges, rows, high_row, DEPTH)
+
+    @pl.when(not_last)
+    def _():
+        rows_down.wait_recv()
+        edges_down.wait_recv()
+        unpack(high_edges, 0, high_row, DEPTH)
+
+    stage_one(-1, 0)
+    stage_one(rows - 1, rows)
+    stage_two(0, quarter - 3)
+    stage_two(3 * quarter + 2, rows - 1)
+    wait_all(back[1])
+    stage_one(quarter - 1, 2 * quarter - 2)
+    stage_two(quarter - 2, 2 * quarter - 3)
+    wait_all(back[2])
+    stage_one(2 * quarter - 1, 3 * quarter)
+    stage_two(2 * quarter - 2, 3 * quarter + 1)
+
     for copy in copies.made:
-        copy.wait_send()
+        if not any(copy is o for o in optional):
+            copy.wait_send()
+
+    @pl.when(first_x)
+    def _():
+        to_last.wait_send()
+        for copy in shear_back[low_row][:-1]:
+            copy.wait_send()
+
+    @pl.when(last_x)
+    def _():
+        to_first.wait_send()
+        for copy in shear_back[high_row][:-1]:
+            copy.wait_send()
+
+    @pl.when(not_first)
+    def _():
+        rows_down.wait_send()
+        edges_down.wait_send()
+
+    @pl.when(not_last)
+    def _():
+        rows_up.wait_send()
+        edges_up.wait_send()
 
 
 def spread(state, residual, shift_rows, shear_offset):
     fields, vertical, rows, cols = state.shape
     groups, radial = lax.axis_size("gy"), lax.axis_size("gx")
     wide = rows + 2 * DEPTH
-    slots = rows + 2 * DEPTH + 2
-    count = 5 * (groups - 1) + 2
+    count = 11 * (groups - 1) + 6
     anywhere = pl.BlockSpec(memory_space=pl.ANY)
     vmem = pl.BlockSpec(memory_space=pltpu.VMEM)
+    edges = pltpu.VMEM((groups, vertical, cols), jnp.float32)
     out = pl.pallas_call(
         functools.partial(spread_kernel, groups, radial),
         out_shape=pltpu.VMEM(state.shape, jnp.float32),
@@ -491,17 +601,18 @@
             pltpu.SMEM(shift_rows.shape, jnp.int32),
             pltpu.SMEM(shear_offset.shape, jnp.int32),
             pltpu.SMEM(residual.shape, jnp.float32),
-            pltpu.VMEM((groups, vertical, rows // 2, cols), jnp.float32),
-            pltpu.VMEM((groups, vertical, rows // 2, cols), jnp.float32),
-            pltpu.VMEM((groups, slots, vertical, cols), jnp.float32),
+            *[pltpu.VMEM((groups, vertical, rows // 4, cols), jnp.float32)] * 4,
+            pltpu.VMEM((groups, rows + DEPTH, vertical, cols), jnp.float32),
+            edges,
             pltpu.VMEM((groups, DEPTH, vertical, cols), jnp.float32),
-            pltpu.VMEM((groups, DEPTH, vertical, cols), jnp.float32),
-            pltpu.VMEM((fields, slots, vertical, cols), jnp.float32),
-            pltpu.VMEM((wide, fields, vertical, 2 * cols), jnp.float32),
+            pltpu.VMEM((fields, wide, vertical, 2 * cols), jnp.float32),
+            edges,
+            edges,
+            edges,
             pltpu.VMEM((wide, fields, vertical, 2 * cols), jnp.float32),
             pltpu.SemaphoreType.DMA((count,)),
             pltpu.SemaphoreType.DMA((count,)),
-            pltpu.SemaphoreType.DMA((8,)),
+            pltpu.SemaphoreType.DMA((14,)),
         ],
         compiler_params=pltpu.CompilerParams(collective_id=1, has_side_effects=True),
     )(state, shift_rows, shear_offset, residual)
@@ -509,7 +620,9 @@
 
 
 def local(state, residual, shift_rows, shear_offset):
-    if lax.axis_size("gy") == state.shape[0] and state.shape[2] % 16 == 0:
+    fields, _, rows, cols = state.shape
+    paired = lax.axis_size("gy") == fields and lax.axis_size("gx") > 2
+    if paired and rows % 16 == 0 and 4 * (rows + DEPTH) <= cols:
         return spread(state, residual, shift_rows, shear_offset)
     return gathered(state, residual, shift_rows, shear_offset)
 

time: 37 us -> 37.9 us (1.024)
  Pallas kernels: 35.1 us -> 36 us
    pallas_call x1, Pallas kernels: 35.1 us -> 36 us  [spread(): pl.pallas_call(functools.partial(spread_kernel, groups, radial), out_shap...]
where the time goes in v2:
time: 37.9 us; the launch traced here: 37.5 us
  Pallas kernels  36 us (95%)
  other arithmetic  0.84 us (2%)
  between operations  0.66 us (2%)
    pallas_call x1, Pallas kernels, spread(): pl.pallas_call(functools.partial(spread_kernel, groups, radial), out_shap...  36 us
    mul x1, other arithmetic, spread(): return 0.5 * out  0.84 us

profile of v2, /device:TPU:0, one launch (start us, length us, event | category | flops | bytes accessed | tf_op | source)
XLA Modules:
  0.0 37.5 jit_solution(10855975584119584768)
XLA Ops:
  0.7 36.0 %shard_map.46 = f32[8,8,16,128]{3,2,1,0:T(8,128)S(1)} custom-call(f32[8,8,16,128]{3,2,1,0:T(8,128)} %state_ref.1, s32[16]{0:T(128)} %shift_hbm.1, s32[1]{0:T(128)S(6)} %copy.5.offset_hbm, f32[64]{0:T(128)} %residual_hbm.1), custom_call_target="tpu_custom_call" | custom-call | tf_op jit(solution)/shard_map/pallas_call | solution.py:595
  36.6 0.8 %broadcast_multiply_fusion = f32[8,8,16,128]{3,2,1,0:T(8,128)} fusion(f32[8,8,16,128]{3,2,1,0:T(8,128)S(1)} %shard_map.46), kind=kLoop, calls=%fused_computation | loop fusion | flops 131072 | bytes 1048576 | tf_op jit(solution)/shard_map/mul | solution.py:619

commit v3 on v2

--- a/solution.py
+++ b/solution.py
@@ -315,25 +315,44 @@
     taken = (taken_0, taken_1, taken_2, taken_3)
     cells_y = cols * groups
     gx, gy = lax.axis_index("gx"), lax.axis_index("gy")
-    copies = Copies(send, recv)
     x_next = (lax.rem(gx + 1, radial), gy)
     x_prev = (lax.rem(gx + radial - 1, radial), gy)
     others = [(gx, lax.rem(gy + k, groups)) for k in range(1, groups)]
     first_x, last_x = gx == 0, gx == radial - 1
-    stays = []
-
-    def stay(source, target):
-        copy = pltpu.make_async_copy(source, target, local_sems.at[len(stays)])
+    not_first, not_last = gx > 0, gx < radial - 1
+    out_sent, back_sent, edges_sent, shear_sent, ends_sent, down_sent, up_sent = range(7)
+    back_got = {0: 4, 3: 5, 1: 6}
+    edges_got, shear_got, ends_got, rows_got, sides_got = 7, 8, 9, (10, 11), (12, 13)
+
+    def remote(source, target, device, sent, got):
+        return pltpu.make_async_remote_copy(
+            src_ref=source,
+            dst_ref=target,
+            send_sem=send.at[sent],
+            recv_sem=recv.at[got],
+            device_id=device,
+            device_id_type=MESH,
+        )
+
+    def spread_out(source, target, sent, got):
+        for other in others:
+            remote(source(other[1]), target, other, sent, got).start()
+        pltpu.make_async_copy(source(gy), target, recv.at[got]).start()
+
+    def arrived(ref, got):
+        pltpu.make_async_copy(ref, ref, recv.at[got]).wait()
+
+    def left(ref, sent):
+        pltpu.make_async_copy(ref, ref, send.at[sent]).wait()
+
+    small = [
+        pltpu.make_async_copy(source, target, local_sems.at[k])
+        for k, (source, target) in enumerate(
+            ((shift_hbm, shift_ref), (offset_hbm, offset_ref), (residual_hbm, residual_ref))
+        )
+    ]
+    for copy in small:
         copy.start()
-        stays.append(copy)
-        return copy
-
-    small = [
-        stay(source, target)
-        for source, target in (
-            (shift_hbm, shift_ref), (offset_hbm, offset_ref), (residual_hbm, residual_ref)
-        )
-    ]
     barrier = pltpu.get_barrier_semaphore()
     for other in (*others, x_prev, x_next):
         pl.semaphore_signal(barrier, inc=1, device_id=other, device_id_type=MESH)
@@ -342,19 +361,16 @@
     def quarter_rows(q):
         return pl.ds(q * quarter, quarter)
 
-    out_flights = {}
-    for q in (0, 3, 1, 2):
-        out_flights[q] = [
-            copies.start(
-                state_ref.at[other[1], :, quarter_rows(q)], taken[q].at[gy], other
-            )
-            for other in others
-        ]
-        out_flights[q].append(stay(state_ref.at[gy, :, quarter_rows(q)], taken[q].at[gy]))
-
-    def wait_all(flights):
-        for copy in flights:
-            copy.wait() if any(copy is s for s in stays) else copy.wait_recv()
+    for pair in ((0, 3), (1, 2)):
+        for other in others:
+            for q in pair:
+                remote(
+                    state_ref.at[other[1], :, quarter_rows(q)], taken[q].at[gy], other, out_sent, q
+                ).start()
+        for q in pair:
+            pltpu.make_async_copy(
+                state_ref.at[gy, :, quarter_rows(q)], taken[q].at[gy], recv.at[q]
+            ).start()
 
     lane = lax.broadcasted_iota(jnp.int32, (vertical, cols), 1)
     empty = [jnp.zeros((vertical, cols), jnp.float32)] * groups
@@ -375,7 +391,7 @@
         return result
 
     def displace_quarter(q, packed):
-        wait_all(out_flights[q])
+        arrived(taken[q], q)
         for place in range(quarter):
             row = q * quarter + place
             packed = displace(
@@ -386,43 +402,35 @@
     def main_lanes(block, first_row, count):
         return moved_ref.at[block, pl.ds(first_row, count), :, pl.ds(0, cols)]
 
-    def send_back(slot, first_row, count):
-        span = pl.ds(slot, count)
-        flights = [
-            copies.start(turned_ref.at[other[1], span], main_lanes(gy, first_row, count), other)
-            for other in others
-        ]
-        flights.append(stay(turned_ref.at[gy, span], main_lanes(gy, first_row, count)))
-        return flights
-
-    def make(source, target, device):
-        k = len(copies.made)
-        copy = pltpu.make_async_remote_copy(
-            src_ref=source,
-            dst_ref=target,
-            send_sem=send.at[k],
-            recv_sem=recv.at[k],
-            device_id=device,
-            device_id_type=MESH,
-        )
-        copies.made.append(copy)
-        optional.append(copy)
-        return copy
-
-    optional = []
+    def send_back(q, count):
+        span = pl.ds(q * quarter, count)
+        spread_out(
+            lambda d: turned_ref.at[d, span],
+            main_lanes(gy, DEPTH + q * quarter, count),
+            back_sent,
+            back_got[q],
+        )
+
     for copy in small:
         copy.wait()
     packed = displace_quarter(0, empty)
-    back = {0: send_back(0, DEPTH, quarter)}
     packed = displace_quarter(3, packed)
-    to_last = make(turned_ref.at[:, pl.ds(0, DEPTH)], shear_ref, x_prev)
-    to_first = make(turned_ref.at[:, pl.ds(rows - DEPTH, DEPTH)], shear_ref, x_next)
+    to_last = remote(turned_ref.at[:, pl.ds(0, DEPTH)], shear_ref, x_prev, ends_sent, ends_got)
+    to_first = remote(
+        turned_ref.at[:, pl.ds(rows - DEPTH, DEPTH)], shear_ref, x_next, ends_sent, ends_got
+    )
     pl.when(first_x)(to_last.start)
     pl.when(last_x)(to_first.start)
-    back[3] = send_back(3 * quarter, DEPTH + 3 * quarter, quarter)
-
-    def sheared(first_row, flight, amount):
-        flight.wait_recv()
+    for q in (0, 3):
+        send_back(q, quarter)
+
+    low_row, high_row = 0, DEPTH + rows
+    offset = offset_ref[0]
+    for d in range(groups):
+        edge_ref[d] = empty[0]
+
+    def sheared(first_row, amount):
+        arrived(shear_ref, ends_got)
         edges = empty
         for place in range(DEPTH):
             edges = displace(
@@ -430,59 +438,44 @@
             )
         for d in range(groups):
             edge_ref[d] = edges[d]
-        for copy in shear_back[first_row]:
-            copy.start()
-
-    span = pl.ds(rows, DEPTH)
-    low_row, high_row = 0, DEPTH + rows
-    shear_back = {}
-    for first_row in (low_row, high_row):
-        shear_back[first_row] = [
-            make(turned_ref.at[other[1], span], main_lanes(gy, first_row, DEPTH), other)
-            for other in others
-        ]
-        copy = pltpu.make_async_copy(
-            turned_ref.at[gy, span], main_lanes(gy, first_row, DEPTH), local_sems.at[len(stays)]
-        )
-        stays.append(copy)
-        shear_back[first_row].append(copy)
-    offset = offset_ref[0]
-    for d in range(groups):
-        edge_ref[d] = empty[0]
+        spread_out(
+            lambda d: turned_ref.at[d, pl.ds(rows, DEPTH)],
+            main_lanes(gy, first_row, DEPTH),
+            shear_sent,
+            shear_got,
+        )
 
     @pl.when(first_x)
     def _():
-        sheared(low_row, to_first, lax.rem(cells_y - offset, cells_y))
+        sheared(low_row, lax.rem(cells_y - offset, cells_y))
 
     @pl.when(last_x)
     def _():
-        sheared(high_row, to_last, offset)
+        sheared(high_row, offset)
 
     packed = displace_quarter(1, packed)
     packed = displace_quarter(2, packed)
     for d in range(groups):
         edge_ref[d] = jnp.where(lane < 4 * rows, packed[d], edge_ref[d])
-    edge_flights = [
-        copies.start(edge_ref.at[other[1]], own_edges.at[gy], other) for other in others
-    ]
-    edge_flights.append(stay(edge_ref.at[gy], own_edges.at[gy]))
-    for q in (1, 2):
-        back[q] = send_back(q * quarter, DEPTH + q * quarter, quarter)
-
+    spread_out(lambda d: edge_ref.at[d], own_edges.at[gy], edges_sent, edges_got)
+    send_back(1, 2 * quarter)
+
+    every = slice(None)
     for q in (0, 3):
-        wait_all(back[q])
-    rows_down = make(
-        main_lanes(slice(None), DEPTH, DEPTH), main_lanes(slice(None), high_row, DEPTH), x_prev
+        arrived(main_lanes(every, DEPTH + q * quarter, quarter), back_got[q])
+    rows_down = remote(
+        main_lanes(every, DEPTH, DEPTH), main_lanes(every, high_row, DEPTH),
+        x_prev, down_sent, rows_got[1],
     )
-    rows_up = make(
-        main_lanes(slice(None), rows, DEPTH), main_lanes(slice(None), low_row, DEPTH), x_next
+    rows_up = remote(
+        main_lanes(every, rows, DEPTH), main_lanes(every, low_row, DEPTH),
+        x_next, up_sent, rows_got[0],
     )
-    edges_down = make(own_edges, high_edges, x_prev)
-    edges_up = make(own_edges, low_edges, x_next)
-    not_first, not_last = gx > 0, gx < radial - 1
+    edges_down = remote(own_edges, high_edges, x_prev, down_sent, sides_got[1])
+    edges_up = remote(own_edges, low_edges, x_next, up_sent, sides_got[0])
     pl.when(not_first)(rows_down.start)
     pl.when(not_last)(rows_up.start)
-    wait_all(edge_flights)
+    arrived(own_edges, edges_got)
     pl.when(not_first)(edges_down.start)
     pl.when(not_last)(edges_up.start)
 
@@ -526,7 +519,7 @@
 
     @pl.when(first_x)
     def _():
-        wait_all(shear_back[low_row])
+        arrived(main_lanes(every, low_row, DEPTH), shear_got)
         unpack(own_edges, rows, low_row, DEPTH)
 
     @pl.when(not_first)
@@ -537,7 +530,7 @@
 
     @pl.when(last_x)
     def _():
-        wait_all(shear_back[high_row])
+        arrived(main_lanes(every, high_row, DEPTH), shear_got)
         unpack(own_edges, rows, high_row, DEPTH)
 
     @pl.when(not_last)
@@ -550,28 +543,19 @@
     stage_one(rows - 1, rows)
     stage_two(0, quarter - 3)
     stage_two(3 * quarter + 2, rows - 1)
-    wait_all(back[1])
-    stage_one(quarter - 1, 2 * quarter - 2)
-    stage_two(quarter - 2, 2 * quarter - 3)
-    wait_all(back[2])
-    stage_one(2 * quarter - 1, 3 * quarter)
-    stage_two(2 * quarter - 2, 3 * quarter + 1)
-
-    for copy in copies.made:
-        if not any(copy is o for o in optional):
-            copy.wait_send()
-
-    @pl.when(first_x)
-    def _():
-        to_last.wait_send()
-        for copy in shear_back[low_row][:-1]:
-            copy.wait_send()
-
-    @pl.when(last_x)
-    def _():
-        to_first.wait_send()
-        for copy in shear_back[high_row][:-1]:
-            copy.wait_send()
+    arrived(main_lanes(every, DEPTH + quarter, 2 * quarter), back_got[1])
+    stage_one(quarter - 1, 3 * quarter)
+    stage_two(quarter - 2, 3 * quarter + 1)
+
+    away = pl.ds(0, groups - 1)
+    left(state_ref.at[away], out_sent)
+    left(turned_ref.at[away, pl.ds(0, rows)], back_sent)
+    left(edge_ref.at[away], edges_sent)
+
+    @pl.when(first_x | last_x)
+    def _():
+        left(shear_ref, ends_sent)
+        left(turned_ref.at[away, pl.ds(rows, DEPTH)], shear_sent)
 
     @pl.when(not_first)
     def _():
@@ -588,7 +572,6 @@
     fields, vertical, rows, cols = state.shape
     groups, radial = lax.axis_size("gy"), lax.axis_size("gx")
     wide = rows + 2 * DEPTH
-    count = 11 * (groups - 1) + 6
     anywhere = pl.BlockSpec(memory_space=pl.ANY)
     vmem = pl.BlockSpec(memory_space=pltpu.VMEM)
     edges = pltpu.VMEM((groups, vertical, cols), jnp.float32)
@@ -610,9 +593,9 @@
             edges,
             edges,
             pltpu.VMEM((wide, fields, vertical, 2 * cols), jnp.float32),
-            pltpu.SemaphoreType.DMA((count,)),
-            pltpu.SemaphoreType.DMA((count,)),
+            pltpu.SemaphoreType.DMA((7,)),
             pltpu.SemaphoreType.DMA((14,)),
+            pltpu.SemaphoreType.DMA((3,)),
         ],
         compiler_params=pltpu.CompilerParams(collective_id=1, has_side_effects=True),
     )(state, shift_rows, shear_offset, residual)

time: 37.9 us -> 36.5 us (0.963)
  the two profiles are of different devices: /device:TPU:0 before, /device:TPU:28 now
where the time goes in v3:
time: 36.5 us; the launch traced here: 36.4 us
  Pallas kernels  34.9 us (96%)
  other arithmetic  0.84 us (2%)
  between operations  0.66 us (2%)
    pallas_call x1, Pallas kernels, spread(): pl.pallas_call(functools.partial(spread_kernel, groups, radial), out_shap...  34.9 us
    mul x1, other arithmetic, spread(): return 0.5 * out  0.84 us

profile of v3, /device:TPU:28, one launch (start us, length us, event | category | flops | bytes accessed | tf_op | source)
XLA Modules:
  0.0 36.4 jit_solution(17505264816619160011)
XLA Ops:
  0.7 34.9 %shard_map.46 = f32[8,8,16,128]{3,2,1,0:T(8,128)S(1)} custom-call(f32[8,8,16,128]{3,2,1,0:T(8,128)} %state_ref.1, s32[16]{0:T(128)} %shift_hbm.1, s32[1]{0:T(128)S(6)} %copy.5.offset_hbm, f32[64]{0:T(128)} %residual_hbm.1), custom_call_target="tpu_custom_call" | custom-call | tf_op jit(solution)/shard_map/pallas_call | solution.py:578
  35.5 0.8 %broadcast_multiply_fusion = f32[8,8,16,128]{3,2,1,0:T(8,128)} fusion(f32[8,8,16,128]{3,2,1,0:T(8,128)S(1)} %shard_map.46), kind=kLoop, calls=%fused_computation | loop fusion | flops 131072 | bytes 1048576 | tf_op jit(solution)/shard_map/mul | solution.py:602

commit v4 on v3

--- a/solution.py
+++ b/solution.py
@@ -16,6 +16,7 @@
 
 MESH = pl.DeviceIdType.MESH
 DEPTH = 2
+WINDOW = 12
 
 
 class Copies:
@@ -308,7 +309,7 @@
 def spread_kernel(
     groups, radial, state_ref, shift_hbm, offset_hbm, residual_hbm, out_ref,
     shift_ref, offset_ref, residual_ref, taken_0, taken_1, taken_2, taken_3, turned_ref, edge_ref,
-    shear_ref, moved_ref, own_edges, low_edges, high_edges, first_ref, send, recv, local_sems,
+    shear_ref, moved_ref, own_edges, low_edges, high_edges, first_ref, windows_ref, drifts_ref, send, recv, local_sems,
 ):
     fields, vertical, rows, cols = state_ref.shape
     quarter = rows // 4
@@ -386,8 +387,10 @@
         result = []
         for d in range(groups):
             turned_ref[d, slot] = row[d]
-            edges = jnp.where(lane < cols // 2, row[(d + 1) % groups], row[d - 1])
-            result.append(jnp.where(mine, pltpu.roll(edges, 4 * place + 2, 1), packed[d]))
+            after = pltpu.roll(row[(d + 1) % groups], 4 * place, 1)
+            before = pltpu.roll(row[d - 1], 4 * place + 4, 1)
+            edges = jnp.where(lane < 4 * place + 2, after, before)
+            result.append(jnp.where(mine, edges, packed[d]))
         return result
 
     def displace_quarter(q, packed):
@@ -400,7 +403,7 @@
         return packed
 
     def main_lanes(block, first_row, count):
-        return moved_ref.at[block, pl.ds(first_row, count), :, pl.ds(0, cols)]
+        return moved_ref.at[block, pl.ds(first_row, count)]
 
     def send_back(q, count):
         span = pl.ds(q * quarter, count)
@@ -458,7 +461,6 @@
     for d in range(groups):
         edge_ref[d] = jnp.where(lane < 4 * rows, packed[d], edge_ref[d])
     spread_out(lambda d: edge_ref.at[d], own_edges.at[gy], edges_sent, edges_got)
-    send_back(1, 2 * quarter)
 
     every = slice(None)
     for q in (0, 3):
@@ -475,18 +477,11 @@
     edges_up = remote(own_edges, low_edges, x_next, up_sent, sides_got[0])
     pl.when(not_first)(rows_down.start)
     pl.when(not_last)(rows_up.start)
+    send_back(1, 2 * quarter)
     arrived(own_edges, edges_got)
     pl.when(not_first)(edges_down.start)
     pl.when(not_last)(edges_up.start)
 
-    def unpack(edges_ref, first_place, first_row, count):
-        for f in range(fields):
-            packed = edges_ref[f]
-            for k in range(count):
-                moved_ref[f, first_row + k, :, cols:] = pltpu.roll(
-                    packed, (cols - 2 - 4 * (first_place + k)) % cols, 1
-                )
-
     start = gx * rows - DEPTH + residual_ref.shape[0]
 
     def drift_of(row):
@@ -498,8 +493,8 @@
 
     def emit_out(row, cur, rates):
         for f in range(fields):
-            second = cur[f][:, :cols] + time_step * rates[f][:, :cols]
-            out_ref[f, :, row - DEPTH, :] = moved_ref[f, row, :, :cols] + second
+            second = cur[f] + time_step * rates[f]
+            out_ref[f, :, row - DEPTH, :] = moved_ref[f, row] + second
 
     def stage_one(low, high):
         row_sweep(
@@ -513,32 +508,106 @@
             DEPTH + low, DEPTH + high, drift_of, emit_out,
         )
 
-    unpack(own_edges, 0, DEPTH, rows)
+    windows = cols // WINDOW
+    kept = windows - 2 * DEPTH
+    starts = range(-DEPTH, rows - DEPTH, kept)
+
+    def in_window(k, low, high):
+        return (lane >= WINDOW * k + low) & (lane < WINDOW * k + high)
+
+    def rows_of(start):
+        return range(start, min(start + windows, rows + DEPTH))
+
+    def window_drift(start):
+        total = empty[0]
+        for k, row in enumerate(rows_of(start)):
+            total = jnp.where(in_window(k, 0, WINDOW), drift_of(DEPTH + row), total)
+        return total
+
+    def fill(i, first_row, count, edges_ref, first_place):
+        for k, row in enumerate(rows_of(starts[i])):
+            if not first_row <= row < first_row + count:
+                continue
+            base, place = WINDOW * k, first_place + row - first_row
+            for f in range(fields):
+                main, edges = moved_ref[f, DEPTH + row], edges_ref[f]
+                value = jnp.where(
+                    in_window(k, 0, 4),
+                    pltpu.roll(main, (base + 4) % cols, 1),
+                    jnp.where(
+                        in_window(k, 4, 8),
+                        pltpu.roll(edges, (base + 4 - 4 * place) % cols, 1),
+                        pltpu.roll(main, (base + 8) % cols, 1),
+                    ),
+                )
+                old = windows_ref[i, f]
+                windows_ref[i, f] = jnp.where(in_window(k, 0, WINDOW), value, old)
+
+    def fill_all(first_row, count, edges_ref, first_place):
+        for i in range(len(starts)):
+            fill(i, first_row, count, edges_ref, first_place)
+
+    def window_step(values, drift):
+        turned = [
+            [pltpu.roll(a, (WINDOW * (1 - r)) % cols, 1) for a in values] for r in range(3)
+        ]
+        drifts = [pltpu.roll(drift, (WINDOW * (1 - r)) % cols, 1) for r in range(3)]
+        got = []
+        row_sweep(
+            lambda r: turned[r], 1, 1, lambda r: drifts[r],
+            lambda r, cur, rates: got.extend(a + time_step * b for a, b in zip(cur, rates)),
+        )
+        return got
+
+    def window_stages(i):
+        drift = drifts_ref[i]
+        moved = [windows_ref[i, f] for f in range(fields)]
+        second = window_step(window_step(moved, drift), drift)
+        outer = (lane < 2) | (lane >= cols - 2)
+        for k, row in enumerate(rows_of(starts[i])):
+            if not DEPTH <= k < DEPTH + kept or row >= rows:
+                continue
+            base = WINDOW * k
+            for f in range(fields):
+                total = moved[f] + second[f]
+                value = jnp.where(
+                    lane < 2,
+                    pltpu.roll(total, (cols - base - 8) % cols, 1),
+                    pltpu.roll(total, (cols - base - 4) % cols, 1),
+                )
+                pltpu.store(out_ref.at[f, :, row, :], value, mask=outer)
+
+    for i in range(len(starts)):
+        drifts_ref[i] = window_drift(starts[i])
+        for f in range(fields):
+            windows_ref[i, f] = empty[0]
     stage_one(1, quarter - 2)
     stage_one(3 * quarter + 1, rows - 2)
 
     @pl.when(first_x)
     def _():
         arrived(main_lanes(every, low_row, DEPTH), shear_got)
-        unpack(own_edges, rows, low_row, DEPTH)
+        fill_all(-DEPTH, DEPTH, own_edges, rows)
 
     @pl.when(not_first)
     def _():
         rows_up.wait_recv()
         edges_up.wait_recv()
-        unpack(low_edges, rows - DEPTH, low_row, DEPTH)
+        fill_all(-DEPTH, DEPTH, low_edges, rows - DEPTH)
 
     @pl.when(last_x)
     def _():
         arrived(main_lanes(every, high_row, DEPTH), shear_got)
-        unpack(own_edges, rows, high_row, DEPTH)
+        fill_all(rows, DEPTH, own_edges, rows)
 
     @pl.when(not_last)
     def _():
         rows_down.wait_recv()
         edges_down.wait_recv()
-        unpack(high_edges, 0, high_row, DEPTH)
-
+        fill_all(rows, DEPTH, high_edges, 0)
+
+    fill_all(0, quarter, own_edges, 0)
+    fill_all(3 * quarter, quarter, own_edges, 3 * quarter)
     stage_one(-1, 0)
     stage_one(rows - 1, rows)
     stage_two(0, quarter - 3)
@@ -546,6 +615,9 @@
     arrived(main_lanes(every, DEPTH + quarter, 2 * quarter), back_got[1])
     stage_one(quarter - 1, 3 * quarter)
     stage_two(quarter - 2, 3 * quarter + 1)
+    fill_all(quarter, 2 * quarter, own_edges, quarter)
+    for i in range(len(starts)):
+        window_stages(i)
 
     away = pl.ds(0, groups - 1)
     left(state_ref.at[away], out_sent)
@@ -572,6 +644,7 @@
     fields, vertical, rows, cols = state.shape
     groups, radial = lax.axis_size("gy"), lax.axis_size("gx")
     wide = rows + 2 * DEPTH
+    parts = len(range(0, rows, cols // WINDOW - 2 * DEPTH))
     anywhere = pl.BlockSpec(memory_space=pl.ANY)
     vmem = pl.BlockSpec(memory_space=pltpu.VMEM)
     edges = pltpu.VMEM((groups, vertical, cols), jnp.float32)
@@ -588,11 +661,13 @@
             pltpu.VMEM((groups, rows + DEPTH, vertical, cols), jnp.float32),
             edges,
             pltpu.VMEM((groups, DEPTH, vertical, cols), jnp.float32),
-            pltpu.VMEM((fields, wide, vertical, 2 * cols), jnp.float32),
+            pltpu.VMEM((fields, wide, vertical, cols), jnp.float32),
             edges,
             edges,
             edges,
-            pltpu.VMEM((wide, fields, vertical, 2 * cols), jnp.float32),
+            pltpu.VMEM((wide, fields, vertical, cols), jnp.float32),
+            pltpu.VMEM((parts, fields, vertical, cols), jnp.float32),
+            pltpu.VMEM((parts, vertical, cols), jnp.float32),
             pltpu.SemaphoreType.DMA((7,)),
             pltpu.SemaphoreType.DMA((14,)),
             pltpu.SemaphoreType.DMA((3,)),

time: 36.5 us -> 36.7 us (level)
  the two profiles are of different devices: /device:TPU:28 before, /device:TPU:0 now
where the time goes in v4:
time: 36.7 us; the launch traced here: 36.5 us
  Pallas kernels  35 us (95%)
  other arithmetic  0.84 us (2%)
  between operations  0.66 us (2%)
    pallas_call x1, Pallas kernels, spread(): pl.pallas_call(functools.partial(spread_kernel, groups, radial), out_shap...  35 us
    mul x1, other arithmetic, spread(): return 0.5 * out  0.84 us

profile of v4, /device:TPU:0, one launch (start us, length us, event | category | flops | bytes accessed | tf_op | source)
XLA Modules:
  0.0 36.5 jit_solution(7185803326232759977)
XLA Ops:
  0.7 35.0 %shard_map.46 = f32[8,8,16,128]{3,2,1,0:T(8,128)S(1)} custom-call(f32[8,8,16,128]{3,2,1,0:T(8,128)} %state_ref.1, s32[16]{0:T(128)} %shift_hbm.1, s32[1]{0:T(128)S(6)} %copy.5.offset_hbm, f32[64]{0:T(128)} %residual_hbm.1), custom_call_target="tpu_custom_call" | custom-call | tf_op jit(solution)/shard_map/pallas_call | solution.py:651
  35.7 0.8 %broadcast_multiply_fusion = f32[8,8,16,128]{3,2,1,0:T(8,128)} fusion(f32[8,8,16,128]{3,2,1,0:T(8,128)S(1)} %shard_map.46), kind=kLoop, calls=%fused_computation | loop fusion | flops 131072 | bytes 1048576 | tf_op jit(solution)/shard_map/mul | solution.py:677

commit v5 on v4

--- a/solution.py
+++ b/solution.py
@@ -212,7 +212,7 @@
         for row in range(first_row, last_row + 1):
             carry = one(row, carry)
         return
-    lax.fori_loop(first_row, last_row + 1, one, carry, unroll=2)
+    lax.fori_loop(first_row, last_row + 1, one, carry, unroll=4)
 
 
 def step_kernel(
@@ -309,7 +309,8 @@
 def spread_kernel(
     groups, radial, state_ref, shift_hbm, offset_hbm, residual_hbm, out_ref,
     shift_ref, offset_ref, residual_ref, taken_0, taken_1, taken_2, taken_3, turned_ref, edge_ref,
-    shear_ref, moved_ref, own_edges, low_edges, high_edges, first_ref, windows_ref, drifts_ref, send, recv, local_sems,
+    shear_ref, moved_ref, own_edges, low_edges, high_edges, first_ref, total_ref, windows_ref,
+    drifts_ref, send, recv, local_sems,
 ):
     fields, vertical, rows, cols = state_ref.shape
     quarter = rows // 4
@@ -487,6 +488,9 @@
     def drift_of(row):
         return residual_ref[lax.rem(start + row, residual_ref.shape[0])]
 
+    windows = cols // WINDOW
+    kept = windows - 2 * DEPTH
+
     def emit_first(row, cur, rates):
         for f in range(fields):
             first_ref[row, f] = cur[f] + time_step * rates[f]
@@ -494,7 +498,18 @@
     def emit_out(row, cur, rates):
         for f in range(fields):
             second = cur[f] + time_step * rates[f]
-            out_ref[f, :, row - DEPTH, :] = moved_ref[f, row] + second
+            total_ref[row - DEPTH, f] = moved_ref[f, row] + second
+
+    def emit_whole(row, cur, rates):
+        i = (row - DEPTH) // kept
+        base = WINDOW * (row - i * kept)
+        for f in range(fields):
+            sides = windows_ref[i, f]
+            low = pltpu.roll(sides, 2 * cols - base - 8, 1)
+            high = pltpu.roll(sides, 2 * cols - base - 4, 1)
+            total = moved_ref[f, row] + (cur[f] + time_step * rates[f])
+            middle = jnp.where(lane >= cols - 2, high, total)
+            out_ref[f, :, row - DEPTH, :] = jnp.where(lane < 2, low, middle)
 
     def stage_one(low, high):
         row_sweep(
@@ -502,14 +517,12 @@
             DEPTH + low, DEPTH + high, drift_of, emit_first,
         )
 
-    def stage_two(low, high):
+    def stage_two(low, high, emit):
         row_sweep(
             lambda row: [first_ref[row, f] for f in range(fields)],
-            DEPTH + low, DEPTH + high, drift_of, emit_out,
-        )
-
-    windows = cols // WINDOW
-    kept = windows - 2 * DEPTH
+            DEPTH + low, DEPTH + high, drift_of, emit,
+        )
+
     starts = range(-DEPTH, rows - DEPTH, kept)
 
     def in_window(k, low, high):
@@ -524,28 +537,25 @@
             total = jnp.where(in_window(k, 0, WINDOW), drift_of(DEPTH + row), total)
         return total
 
-    def fill(i, first_row, count, edges_ref, first_place):
-        for k, row in enumerate(rows_of(starts[i])):
-            if not first_row <= row < first_row + count:
-                continue
-            base, place = WINDOW * k, first_place + row - first_row
-            for f in range(fields):
-                main, edges = moved_ref[f, DEPTH + row], edges_ref[f]
-                value = jnp.where(
-                    in_window(k, 0, 4),
-                    pltpu.roll(main, (base + 4) % cols, 1),
-                    jnp.where(
-                        in_window(k, 4, 8),
-                        pltpu.roll(edges, (base + 4 - 4 * place) % cols, 1),
-                        pltpu.roll(main, (base + 8) % cols, 1),
-                    ),
-                )
-                old = windows_ref[i, f]
-                windows_ref[i, f] = jnp.where(in_window(k, 0, WINDOW), value, old)
-
     def fill_all(first_row, count, edges_ref, first_place):
         for i in range(len(starts)):
-            fill(i, first_row, count, edges_ref, first_place)
+            held = [
+                (k, row) for k, row in enumerate(rows_of(starts[i]))
+                if first_row <= row < first_row + count
+            ]
+            for f in range(fields):
+                packed, value = edges_ref[f], windows_ref[i, f]
+                for k, row in held:
+                    base, place = WINDOW * k, first_place + row - first_row
+                    main = moved_ref[f, DEPTH + row]
+                    for low, source, turn in (
+                        (0, main, base + 4), (4, packed, base + 4 - 4 * place), (8, main, base + 8)
+                    ):
+                        value = jnp.where(
+                            in_window(k, low, low + 4), pltpu.roll(source, turn % cols, 1), value
+                        )
+                if held:
+                    windows_ref[i, f] = value
 
     def window_step(values, drift):
         turned = [
@@ -563,19 +573,18 @@
         drift = drifts_ref[i]
         moved = [windows_ref[i, f] for f in range(fields)]
         second = window_step(window_step(moved, drift), drift)
-        outer = (lane < 2) | (lane >= cols - 2)
-        for k, row in enumerate(rows_of(starts[i])):
-            if not DEPTH <= k < DEPTH + kept or row >= rows:
-                continue
-            base = WINDOW * k
-            for f in range(fields):
-                total = moved[f] + second[f]
-                value = jnp.where(
-                    lane < 2,
-                    pltpu.roll(total, (cols - base - 8) % cols, 1),
-                    pltpu.roll(total, (cols - base - 4) % cols, 1),
-                )
-                pltpu.store(out_ref.at[f, :, row, :], value, mask=outer)
+        for f in range(fields):
+            windows_ref[i, f] = moved[f] + second[f]
+
+    def finish(row):
+        i = row // kept
+        base = WINDOW * (row - i * kept + DEPTH)
+        for f in range(fields):
+            sides = windows_ref[i, f]
+            low = pltpu.roll(sides, (cols - base - 8) % cols, 1)
+            high = pltpu.roll(sides, (cols - base - 4) % cols, 1)
+            middle = jnp.where(lane >= cols - 2, high, total_ref[row, f])
+            out_ref[f, :, row, :] = jnp.where(lane < 2, low, middle)
 
     for i in range(len(starts)):
         drifts_ref[i] = window_drift(starts[i])
@@ -610,14 +619,16 @@
     fill_all(3 * quarter, quarter, own_edges, 3 * quarter)
     stage_one(-1, 0)
     stage_one(rows - 1, rows)
-    stage_two(0, quarter - 3)
-    stage_two(3 * quarter + 2, rows - 1)
+    stage_two(0, quarter - 3, emit_out)
+    stage_two(3 * quarter + 2, rows - 1, emit_out)
     arrived(main_lanes(every, DEPTH + quarter, 2 * quarter), back_got[1])
-    stage_one(quarter - 1, 3 * quarter)
-    stage_two(quarter - 2, 3 * quarter + 1)
     fill_all(quarter, 2 * quarter, own_edges, quarter)
     for i in range(len(starts)):
         window_stages(i)
+    stage_one(quarter - 1, 3 * quarter)
+    stage_two(quarter - 2, 3 * quarter + 1, emit_whole)
+    for row in (*range(quarter - 2), *range(3 * quarter + 2, rows)):
+        finish(row)
 
     away = pl.ds(0, groups - 1)
     left(state_ref.at[away], out_sent)
@@ -666,6 +677,7 @@
             edges,
             edges,
             pltpu.VMEM((wide, fields, vertical, cols), jnp.float32),
+            pltpu.VMEM((rows, fields, vertical, cols), jnp.float32),
             pltpu.VMEM((parts, fields, vertical, cols), jnp.float32),
             pltpu.VMEM((parts, vertical, cols), jnp.float32),
             pltpu.SemaphoreType.DMA((7,)),

time: 36.7 us -> 35.7 us (0.973)
  Pallas kernels: 35 us -> 34 us
    pallas_call x1, Pallas kernels: 35 us -> 34 us  [spread(): pl.pallas_call(functools.partial(spread_kernel, groups, radial), out_shap...]
where the time goes in v5:
time: 35.7 us; the launch traced here: 35.5 us
  Pallas kernels  34 us (95%)
  other arithmetic  0.84 us (2%)
  between operations  0.66 us (2%)
    pallas_call x1, Pallas kernels, spread(): pl.pallas_call(functools.partial(spread_kernel, groups, radial), out_shap...  34 us
    mul x1, other arithmetic, spread(): return 0.5 * out  0.84 us

profile of v5, /device:TPU:0, one launch (start us, length us, event | category | flops | bytes accessed | tf_op | source)
XLA Modules:
  0.0 35.5 jit_solution(5184771905505025847)
XLA Ops:
  0.7 34.0 %shard_map.46 = f32[8,8,16,128]{3,2,1,0:T(8,128)S(1)} custom-call(f32[8,8,16,128]{3,2,1,0:T(8,128)} %state_ref.1, s32[16]{0:T(128)} %shift_hbm.1, s32[1]{0:T(128)S(6)} %copy.5.offset_hbm, f32[64]{0:T(128)} %residual_hbm.1), custom_call_target="tpu_custom_call" | custom-call | tf_op jit(solution)/shard_map/pallas_call | solution.py:662
  34.7 0.8 %broadcast_multiply_fusion = f32[8,8,16,128]{3,2,1,0:T(8,128)} fusion(f32[8,8,16,128]{3,2,1,0:T(8,128)S(1)} %shard_map.46), kind=kLoop, calls=%fused_computation | loop fusion | flops 131072 | bytes 1048576 | tf_op jit(solution)/shard_map/mul | solution.py:689

commit v6 on v5

--- a/solution.py
+++ b/solution.py
@@ -17,6 +17,11 @@
 MESH = pl.DeviceIdType.MESH
 DEPTH = 2
 WINDOW = 12
+EARLY = (1, 0)
+
+
+def late_rows(rows):
+    return range(rows // 4 + EARLY[0], 3 * rows // 4 - EARLY[1])
 
 
 class Copies:
@@ -309,12 +314,16 @@
 def spread_kernel(
     groups, radial, state_ref, shift_hbm, offset_hbm, residual_hbm, out_ref,
     shift_ref, offset_ref, residual_ref, taken_0, taken_1, taken_2, taken_3, turned_ref, edge_ref,
-    shear_ref, moved_ref, own_edges, low_edges, high_edges, first_ref, total_ref, windows_ref,
-    drifts_ref, send, recv, local_sems,
+    shear_ref, moved_ref, own_edges, low_edges, high_edges, first_ref, windows_ref, drifts_ref, send, recv, local_sems,
 ):
     fields, vertical, rows, cols = state_ref.shape
     quarter = rows // 4
     taken = (taken_0, taken_1, taken_2, taken_3)
+    late = late_rows(rows)
+    others_start = WINDOW * len(late)
+    short = [row for row in range(rows + DEPTH) if row not in late]
+    lane_of = {row: WINDOW * k for k, row in enumerate(late)}
+    lane_of.update({row: others_start + 4 * k for k, row in enumerate(short)})
     cells_y = cols * groups
     gx, gy = lax.axis_index("gx"), lax.axis_index("gy")
     x_next = (lax.rem(gx + 1, radial), gy)
@@ -323,7 +332,7 @@
     first_x, last_x = gx == 0, gx == radial - 1
     not_first, not_last = gx > 0, gx < radial - 1
     out_sent, back_sent, edges_sent, shear_sent, ends_sent, down_sent, up_sent = range(7)
-    back_got = {0: 4, 3: 5, 1: 6}
+    back_got = (4, 5, 6, 14, 15)
     edges_got, shear_got, ends_got, rows_got, sides_got = 7, 8, 9, (10, 11), (12, 13)
 
     def remote(source, target, device, sent, got):
@@ -377,20 +386,29 @@
     lane = lax.broadcasted_iota(jnp.int32, (vertical, cols), 1)
     empty = [jnp.zeros((vertical, cols), jnp.float32)] * groups
 
-    def displace(block_of, amount, place, slot, packed):
+    def displace(block_of, amount, slot, packed):
         whole, part = amount // cols, amount % cols
         rolled = [
             pltpu.roll(block_of(lax.rem(k - whole + groups, groups)), part, 1)
             for k in range(groups)
         ]
         row = [jnp.where(lane < part, rolled[d - 1], rolled[d]) for d in range(groups)]
-        mine = (lane >= 4 * place) & (lane < 4 * place + 4)
+        base, long = lane_of[slot], slot in late
+        width = WINDOW if long else 4
+        mine = (lane >= base) & (lane < base + width)
         result = []
         for d in range(groups):
             turned_ref[d, slot] = row[d]
-            after = pltpu.roll(row[(d + 1) % groups], 4 * place, 1)
-            before = pltpu.roll(row[d - 1], 4 * place + 4, 1)
-            edges = jnp.where(lane < 4 * place + 2, after, before)
+            before, here, after = row[d - 1], row[d], row[(d + 1) % groups]
+            if long:
+                after = jnp.where(lane < cols // 2, after, here)
+                before = jnp.where(lane < cols // 2, here, before)
+            turn = base + 4
+            edges = jnp.where(
+                lane < base + width // 2,
+                pltpu.roll(after, turn % cols if long else base, 1),
+                pltpu.roll(before, (base + width - 4 if long else base + 4) % cols, 1),
+            )
             result.append(jnp.where(mine, edges, packed[d]))
         return result
 
@@ -399,21 +417,35 @@
         for place in range(quarter):
             row = q * quarter + place
             packed = displace(
-                lambda b: taken[q][b, :, place, :], shift_ref[row], row, row, packed
+                lambda b: taken[q][b, :, place, :], shift_ref[row], row, packed
             )
         return packed
 
     def main_lanes(block, first_row, count):
         return moved_ref.at[block, pl.ds(first_row, count)]
 
-    def send_back(q, count):
-        span = pl.ds(q * quarter, count)
-        spread_out(
-            lambda d: turned_ref.at[d, span],
-            main_lanes(gy, DEPTH + q * quarter, count),
-            back_sent,
-            back_got[q],
-        )
+    pieces = (
+        (0, quarter),
+        (3 * quarter, quarter),
+        (quarter, EARLY[0]),
+        (3 * quarter - EARLY[1], EARLY[1]),
+        (late[0], len(late)),
+    )
+
+    def send_back(piece):
+        first, count = pieces[piece]
+        if count:
+            spread_out(
+                lambda d: turned_ref.at[d, pl.ds(first, count)],
+                main_lanes(gy, DEPTH + first, count),
+                back_sent,
+                back_got[piece],
+            )
+
+    def wait_back(piece):
+        first, count = pieces[piece]
+        if count:
+            arrived(main_lanes(slice(None), DEPTH + first, count), back_got[piece])
 
     for copy in small:
         copy.wait()
@@ -425,8 +457,8 @@
     )
     pl.when(first_x)(to_last.start)
     pl.when(last_x)(to_first.start)
-    for q in (0, 3):
-        send_back(q, quarter)
+    for piece in (0, 1):
+        send_back(piece)
 
     low_row, high_row = 0, DEPTH + rows
     offset = offset_ref[0]
@@ -438,7 +470,7 @@
         edges = empty
         for place in range(DEPTH):
             edges = displace(
-                lambda b: shear_ref[b, place], amount, rows + place, rows + place, edges
+                lambda b: shear_ref[b, place], amount, rows + place, edges
             )
         for d in range(groups):
             edge_ref[d] = edges[d]
@@ -460,12 +492,14 @@
     packed = displace_quarter(1, packed)
     packed = displace_quarter(2, packed)
     for d in range(groups):
-        edge_ref[d] = jnp.where(lane < 4 * rows, packed[d], edge_ref[d])
+        edge_ref[d] = jnp.where(lane < lane_of[rows], packed[d], edge_ref[d])
     spread_out(lambda d: edge_ref.at[d], own_edges.at[gy], edges_sent, edges_got)
+    for piece in (2, 3):
+        send_back(piece)
 
     every = slice(None)
-    for q in (0, 3):
-        arrived(main_lanes(every, DEPTH + q * quarter, quarter), back_got[q])
+    for piece in (0, 1):
+        wait_back(piece)
     rows_down = remote(
         main_lanes(every, DEPTH, DEPTH), main_lanes(every, high_row, DEPTH),
         x_prev, down_sent, rows_got[1],
@@ -478,7 +512,7 @@
     edges_up = remote(own_edges, low_edges, x_next, up_sent, sides_got[0])
     pl.when(not_first)(rows_down.start)
     pl.when(not_last)(rows_up.start)
-    send_back(1, 2 * quarter)
+    send_back(4)
     arrived(own_edges, edges_got)
     pl.when(not_first)(edges_down.start)
     pl.when(not_last)(edges_up.start)
@@ -494,11 +528,6 @@
     def emit_first(row, cur, rates):
         for f in range(fields):
             first_ref[row, f] = cur[f] + time_step * rates[f]
-
-    def emit_out(row, cur, rates):
-        for f in range(fields):
-            second = cur[f] + time_step * rates[f]
-            total_ref[row - DEPTH, f] = moved_ref[f, row] + second
 
     def emit_whole(row, cur, rates):
         i = (row - DEPTH) // kept
@@ -517,10 +546,10 @@
             DEPTH + low, DEPTH + high, drift_of, emit_first,
         )
 
-    def stage_two(low, high, emit):
+    def stage_two(low, high):
         row_sweep(
             lambda row: [first_ref[row, f] for f in range(fields)],
-            DEPTH + low, DEPTH + high, drift_of, emit,
+            DEPTH + low, DEPTH + high, drift_of, emit_whole,
         )
 
     starts = range(-DEPTH, rows - DEPTH, kept)
@@ -541,21 +570,32 @@
         for i in range(len(starts)):
             held = [
                 (k, row) for k, row in enumerate(rows_of(starts[i]))
-                if first_row <= row < first_row + count
+                if first_row <= row < first_row + count and row not in late
             ]
             for f in range(fields):
                 packed, value = edges_ref[f], windows_ref[i, f]
                 for k, row in held:
-                    base, place = WINDOW * k, first_place + row - first_row
+                    base, from_lane = WINDOW * k, lane_of[first_place + row - first_row]
                     main = moved_ref[f, DEPTH + row]
                     for low, source, turn in (
-                        (0, main, base + 4), (4, packed, base + 4 - 4 * place), (8, main, base + 8)
+                        (0, main, base + 4), (4, packed, base + 4 - from_lane), (8, main, base + 8)
                     ):
                         value = jnp.where(
                             in_window(k, low, low + 4), pltpu.roll(source, turn % cols, 1), value
                         )
                 if held:
                     windows_ref[i, f] = value
+
+    def fill_late():
+        for i in range(len(starts)):
+            held = [k for k, row in enumerate(rows_of(starts[i])) if row in late]
+            if not held:
+                continue
+            from_lane = lane_of[starts[i] + held[0]]
+            mine = (lane >= WINDOW * held[0]) & (lane < WINDOW * (held[-1] + 1))
+            for f in range(fields):
+                value = pltpu.roll(own_edges[f], (WINDOW * held[0] - from_lane) % cols, 1)
+                windows_ref[i, f] = jnp.where(mine, value, windows_ref[i, f])
 
     def window_step(values, drift):
         turned = [
@@ -576,22 +616,16 @@
         for f in range(fields):
             windows_ref[i, f] = moved[f] + second[f]
 
-    def finish(row):
-        i = row // kept
-        base = WINDOW * (row - i * kept + DEPTH)
-        for f in range(fields):
-            sides = windows_ref[i, f]
-            low = pltpu.roll(sides, (cols - base - 8) % cols, 1)
-            high = pltpu.roll(sides, (cols - base - 4) % cols, 1)
-            middle = jnp.where(lane >= cols - 2, high, total_ref[row, f])
-            out_ref[f, :, row, :] = jnp.where(lane < 2, low, middle)
-
     for i in range(len(starts)):
         drifts_ref[i] = window_drift(starts[i])
         for f in range(fields):
             windows_ref[i, f] = empty[0]
-    stage_one(1, quarter - 2)
-    stage_one(3 * quarter + 1, rows - 2)
+    fill_late()
+    for piece in (2, 3):
+        wait_back(piece)
+    fill_all(0, rows, own_edges, 0)
+    stage_one(1, late[0] - 2)
+    stage_one(late[-1] + 2, rows - 2)
 
     @pl.when(first_x)
     def _():
@@ -615,20 +649,15 @@
         edges_down.wait_recv()
         fill_all(rows, DEPTH, high_edges, 0)
 
-    fill_all(0, quarter, own_edges, 0)
-    fill_all(3 * quarter, quarter, own_edges, 3 * quarter)
+    for i in range(len(starts)):
+        window_stages(i)
     stage_one(-1, 0)
     stage_one(rows - 1, rows)
-    stage_two(0, quarter - 3, emit_out)
-    stage_two(3 * quarter + 2, rows - 1, emit_out)
-    arrived(main_lanes(every, DEPTH + quarter, 2 * quarter), back_got[1])
-    fill_all(quarter, 2 * quarter, own_edges, quarter)
-    for i in range(len(starts)):
-        window_stages(i)
-    stage_one(quarter - 1, 3 * quarter)
-    stage_two(quarter - 2, 3 * quarter + 1, emit_whole)
-    for row in (*range(quarter - 2), *range(3 * quarter + 2, rows)):
-        finish(row)
+    stage_two(0, late[0] - 3)
+    stage_two(late[-1] + 3, rows - 1)
+    wait_back(4)
+    stage_one(late[0] - 1, late[-1] + 1)
+    stage_two(late[0] - 2, late[-1] + 2)
 
     away = pl.ds(0, groups - 1)
     left(state_ref.at[away], out_sent)
@@ -677,11 +706,10 @@
             edges,
             edges,
             pltpu.VMEM((wide, fields, vertical, cols), jnp.float32),
-            pltpu.VMEM((rows, fields, vertical, cols), jnp.float32),
             pltpu.VMEM((parts, fields, vertical, cols), jnp.float32),
             pltpu.VMEM((parts, vertical, cols), jnp.float32),
             pltpu.SemaphoreType.DMA((7,)),
-            pltpu.SemaphoreType.DMA((14,)),
+            pltpu.SemaphoreType.DMA((16,)),
             pltpu.SemaphoreType.DMA((3,)),
         ],
         compiler_params=pltpu.CompilerParams(collective_id=1, has_side_effects=True),
@@ -692,7 +720,8 @@
 def local(state, residual, shift_rows, shear_offset):
     fields, _, rows, cols = state.shape
     paired = lax.axis_size("gy") == fields and lax.axis_size("gx") > 2
-    if paired and rows % 16 == 0 and 4 * (rows + DEPTH) <= cols:
+    late = len(late_rows(rows))
+    if paired and rows % 16 == 0 and WINDOW * late + 4 * (rows + DEPTH - late) <= cols:
         return spread(state, residual, shift_rows, shear_offset)
     return gathered(state, residual, shift_rows, shear_offset)
 

time: 35.7 us -> 35.3 us (0.989)
  Pallas kernels: 34 us -> 33.6 us
    pallas_call x1, Pallas kernels: 34 us -> 33.6 us  [spread(): pl.pallas_call(functools.partial(spread_kernel, groups, radial), out_shap...]
where the time goes in v6:
time: 35.3 us; the launch traced here: 35.1 us
  Pallas kernels  33.6 us (95%)
  other arithmetic  0.84 us (2%)
  between operations  0.66 us (2%)
    pallas_call x1, Pallas kernels, spread(): pl.pallas_call(functools.partial(spread_kernel, groups, radial), out_shap...  33.6 us
    mul x1, other arithmetic, spread(): return 0.5 * out  0.84 us

profile of v6, /device:TPU:0, one launch (start us, length us, event | category | flops | bytes accessed | tf_op | source)
XLA Modules:
  0.0 35.1 jit_solution(16312619414955104087)
XLA Ops:
  0.7 33.6 %shard_map.46 = f32[8,8,16,128]{3,2,1,0:T(8,128)S(1)} custom-call(f32[8,8,16,128]{3,2,1,0:T(8,128)} %state_ref.1, s32[16]{0:T(128)} %shift_hbm.1, s32[1]{0:T(128)S(6)} %copy.5.offset_hbm, f32[64]{0:T(128)} %residual_hbm.1), custom_call_target="tpu_custom_call" | custom-call | tf_op jit(solution)/shard_map/pallas_call | solution.py:691
  34.3 0.8 %broadcast_multiply_fusion = f32[8,8,16,128]{3,2,1,0:T(8,128)} fusion(f32[8,8,16,128]{3,2,1,0:T(8,128)S(1)} %shard_map.46), kind=kLoop, calls=%fused_computation | loop fusion | flops 131072 | bytes 1048576 | tf_op jit(solution)/shard_map/mul | solution.py:717

commit v7 on v6

--- a/solution.py
+++ b/solution.py
@@ -124,7 +124,7 @@
         copy.wait_send()
 
 
-def row_sweep(load, first_row, last_row, drift_of, emit):
+def row_sweep(load, first_row, last_row, drift_of, emit, unroll=4):
     def y_ahead(a):
         return pltpu.roll(a, a.shape[1] - 1, 1)
 
@@ -217,7 +217,7 @@
         for row in range(first_row, last_row + 1):
             carry = one(row, carry)
         return
-    lax.fori_loop(first_row, last_row + 1, one, carry, unroll=4)
+    lax.fori_loop(first_row, last_row + 1, one, carry, unroll=unroll)
 
 
 def step_kernel(
@@ -543,13 +543,13 @@
     def stage_one(low, high):
         row_sweep(
             lambda row: [moved_ref[f, row] for f in range(fields)],
-            DEPTH + low, DEPTH + high, drift_of, emit_first,
+            DEPTH + low, DEPTH + high, drift_of, emit_first, 3,
         )
 
     def stage_two(low, high):
         row_sweep(
             lambda row: [first_ref[row, f] for f in range(fields)],
-            DEPTH + low, DEPTH + high, drift_of, emit_whole,
+            DEPTH + low, DEPTH + high, drift_of, emit_whole, 4,
         )
 
     starts = range(-DEPTH, rows - DEPTH, kept)
@@ -624,6 +624,9 @@
     for piece in (2, 3):
         wait_back(piece)
     fill_all(0, rows, own_edges, 0)
+    inside = [i for i in range(len(starts)) if starts[i] >= 0 and rows_of(starts[i])[-1] < rows]
+    for i in inside:
+        window_stages(i)
     stage_one(1, late[0] - 2)
     stage_one(late[-1] + 2, rows - 2)
 
@@ -632,27 +635,29 @@
         arrived(main_lanes(every, low_row, DEPTH), shear_got)
         fill_all(-DEPTH, DEPTH, own_edges, rows)
 
+    @pl.when(last_x)
+    def _():
+        arrived(main_lanes(every, high_row, DEPTH), shear_got)
+        fill_all(rows, DEPTH, own_edges, rows)
+
+    pl.when(not_first)(rows_up.wait_recv)
+    pl.when(not_last)(rows_down.wait_recv)
+    stage_one(-1, 0)
+    stage_one(rows - 1, rows)
+
     @pl.when(not_first)
     def _():
-        rows_up.wait_recv()
         edges_up.wait_recv()
         fill_all(-DEPTH, DEPTH, low_edges, rows - DEPTH)
 
-    @pl.when(last_x)
-    def _():
-        arrived(main_lanes(every, high_row, DEPTH), shear_got)
-        fill_all(rows, DEPTH, own_edges, rows)
-
     @pl.when(not_last)
     def _():
-        rows_down.wait_recv()
         edges_down.wait_recv()
         fill_all(rows, DEPTH, high_edges, 0)
 
     for i in range(len(starts)):
-        window_stages(i)
-    stage_one(-1, 0)
-    stage_one(rows - 1, rows)
+        if i not in inside:
+            window_stages(i)
     stage_two(0, late[0] - 3)
     stage_two(late[-1] + 3, rows - 1)
     wait_back(4)

time: 35.3 us -> 34.5 us (0.977)
  Pallas kernels: 33.6 us -> 32.8 us
    pallas_call x1, Pallas kernels: 33.6 us -> 32.8 us  [spread(): pl.pallas_call(functools.partial(spread_kernel, groups, radial), out_shap...]
where the time goes in v7:
time: 34.5 us; the launch traced here: 34.3 us
  Pallas kernels  32.8 us (95%)
  other arithmetic  0.84 us (2%)
  between operations  0.66 us (2%)
    pallas_call x1, Pallas kernels, spread(): pl.pallas_call(functools.partial(spread_kernel, groups, radial), out_shap...  32.8 us
    mul x1, other arithmetic, spread(): return 0.5 * out  0.84 us

profile of v7, /device:TPU:0, one launch (start us, length us, event | category | flops | bytes accessed | tf_op | source)
XLA Modules:
  0.0 34.3 jit_solution(12679344063770600046)
XLA Ops:
  0.7 32.8 %shard_map.46 = f32[8,8,16,128]{3,2,1,0:T(8,128)S(1)} custom-call(f32[8,8,16,128]{3,2,1,0:T(8,128)} %state_ref.1, s32[16]{0:T(128)} %shift_hbm.1, s32[1]{0:T(128)S(6)} %copy.5.offset_hbm, f32[64]{0:T(128)} %residual_hbm.1), custom_call_target="tpu_custom_call" | custom-call | tf_op jit(solution)/shard_map/pallas_call | solution.py:696
  33.5 0.8 %broadcast_multiply_fusion = f32[8,8,16,128]{3,2,1,0:T(8,128)} fusion(f32[8,8,16,128]{3,2,1,0:T(8,128)S(1)} %shard_map.46), kind=kLoop, calls=%fused_computation | loop fusion | flops 131072 | bytes 1048576 | tf_op jit(solution)/shard_map/mul | solution.py:722

commit v8 on v7

--- a/solution.py
+++ b/solution.py
@@ -332,7 +332,7 @@
     first_x, last_x = gx == 0, gx == radial - 1
     not_first, not_last = gx > 0, gx < radial - 1
     out_sent, back_sent, edges_sent, shear_sent, ends_sent, down_sent, up_sent = range(7)
-    back_got = (4, 5, 6, 14, 15)
+    back_got = (4, 5, 6, 14, 15, 16)
     edges_got, shear_got, ends_got, rows_got, sides_got = 7, 8, 9, (10, 11), (12, 13)
 
     def remote(source, target, device, sent, got):
@@ -429,7 +429,8 @@
         (3 * quarter, quarter),
         (quarter, EARLY[0]),
         (3 * quarter - EARLY[1], EARLY[1]),
-        (late[0], len(late)),
+        (late[0], len(late) // 2),
+        (late[len(late) // 2], len(late) - len(late) // 2),
     )
 
     def send_back(piece):
@@ -513,6 +514,7 @@
     pl.when(not_first)(rows_down.start)
     pl.when(not_last)(rows_up.start)
     send_back(4)
+    send_back(5)
     arrived(own_edges, edges_got)
     pl.when(not_first)(edges_down.start)
     pl.when(not_last)(edges_up.start)
@@ -661,8 +663,12 @@
     stage_two(0, late[0] - 3)
     stage_two(late[-1] + 3, rows - 1)
     wait_back(4)
-    stage_one(late[0] - 1, late[-1] + 1)
-    stage_two(late[0] - 2, late[-1] + 2)
+    middle = late[len(late) // 2]
+    stage_one(late[0] - 1, middle - 2)
+    stage_two(late[0] - 2, middle - 3)
+    wait_back(5)
+    stage_one(middle - 1, late[-1] + 1)
+    stage_two(middle - 2, late[-1] + 2)
 
     away = pl.ds(0, groups - 1)
     left(state_ref.at[away], out_sent)
@@ -714,7 +720,7 @@
             pltpu.VMEM((parts, fields, vertical, cols), jnp.float32),
             pltpu.VMEM((parts, vertical, cols), jnp.float32),
             pltpu.SemaphoreType.DMA((7,)),
-            pltpu.SemaphoreType.DMA((16,)),
+            pltpu.SemaphoreType.DMA((17,)),
             pltpu.SemaphoreType.DMA((3,)),
         ],
         compiler_params=pltpu.CompilerParams(collective_id=1, has_side_effects=True),

time: 34.5 us -> 34.3 us (level)
  no operation moved by 1% of the time
where the time goes in v8:
time: 34.3 us; the launch traced here: 34.1 us
  Pallas kernels  32.6 us (95%)
  other arithmetic  0.84 us (2%)
  between operations  0.66 us (2%)
    pallas_call x1, Pallas kernels, spread(): pl.pallas_call(functools.partial(spread_kernel, groups, radial), out_shap...  32.6 us
    mul x1, other arithmetic, spread(): return 0.5 * out  0.84 us

profile of v8, /device:TPU:0, one launch (start us, length us, event | category | flops | bytes accessed | tf_op | source)
XLA Modules:
  0.0 34.1 jit_solution(17008912857619463199)
XLA Ops:
  0.7 32.6 %shard_map.46 = f32[8,8,16,128]{3,2,1,0:T(8,128)S(1)} custom-call(f32[8,8,16,128]{3,2,1,0:T(8,128)} %state_ref.1, s32[16]{0:T(128)} %shift_hbm.1, s32[1]{0:T(128)S(6)} %copy.5.offset_hbm, f32[64]{0:T(128)} %residual_hbm.1), custom_call_target="tpu_custom_call" | custom-call | tf_op jit(solution)/shard_map/pallas_call | solution.py:702
  33.3 0.8 %broadcast_multiply_fusion = f32[8,8,16,128]{3,2,1,0:T(8,128)} fusion(f32[8,8,16,128]{3,2,1,0:T(8,128)S(1)} %shard_map.46), kind=kLoop, calls=%fused_computation | loop fusion | flops 131072 | bytes 1048576 | tf_op jit(solution)/shard_map/mul | solution.py:728

commit v9 on v8

--- a/solution.py
+++ b/solution.py
@@ -124,7 +124,7 @@
         copy.wait_send()
 
 
-def row_sweep(load, first_row, last_row, drift_of, emit, unroll=4):
+def row_sweep(load, first_row, last_row, drift_of, emit, unroll=4, base=0):
     def y_ahead(a):
         return pltpu.roll(a, a.shape[1] - 1, 1)
 
@@ -213,9 +213,9 @@
         emit(row, cur, rates)
         return cy, cz, cy_next, cz_next, emf_z_next, emf_y_next
 
-    if last_row - first_row < 3:
+    if last_row - first_row < 6:
         for row in range(first_row, last_row + 1):
-            carry = one(row, carry)
+            carry = one(row + base, carry)
         return
     lax.fori_loop(first_row, last_row + 1, one, carry, unroll=unroll)
 
@@ -330,6 +330,7 @@
     x_prev = (lax.rem(gx + radial - 1, radial), gy)
     others = [(gx, lax.rem(gy + k, groups)) for k in range(1, groups)]
     first_x, last_x = gx == 0, gx == radial - 1
+    zero = gx // radial
     not_first, not_last = gx > 0, gx < radial - 1
     out_sent, back_sent, edges_sent, shear_sent, ends_sent, down_sent, up_sent = range(7)
     back_got = (4, 5, 6, 14, 15, 16)
@@ -545,13 +546,13 @@
     def stage_one(low, high):
         row_sweep(
             lambda row: [moved_ref[f, row] for f in range(fields)],
-            DEPTH + low, DEPTH + high, drift_of, emit_first, 3,
+            DEPTH + low, DEPTH + high, drift_of, emit_first, 3, zero,
         )
 
     def stage_two(low, high):
         row_sweep(
             lambda row: [first_ref[row, f] for f in range(fields)],
-            DEPTH + low, DEPTH + high, drift_of, emit_whole, 4,
+            DEPTH + low, DEPTH + high, drift_of, emit_whole, 4, zero,
         )
 
     starts = range(-DEPTH, rows - DEPTH, kept)

time: 34.3 us -> 34.2 us (level)
  no operation moved by 1% of the time
where the time goes in v9:
time: 34.2 us; the launch traced here: 34 us
  Pallas kernels  32.5 us (95%)
  other arithmetic  0.84 us (2%)
  between operations  0.66 us (2%)
    pallas_call x1, Pallas kernels, spread(): pl.pallas_call(functools.partial(spread_kernel, groups, radial), out_shap...  32.5 us
    mul x1, other arithmetic, spread(): return 0.5 * out  0.84 us

profile of v9, /device:TPU:0, one launch (start us, length us, event | category | flops | bytes accessed | tf_op | source)
XLA Modules:
  0.0 34.0 jit_solution(6676955410272949679)
XLA Ops:
  0.7 32.5 %shard_map.46 = f32[8,8,16,128]{3,2,1,0:T(8,128)S(1)} custom-call(f32[8,8,16,128]{3,2,1,0:T(8,128)} %state_ref.1, s32[16]{0:T(128)} %shift_hbm.1, s32[1]{0:T(128)S(6)} %copy.5.offset_hbm, f32[64]{0:T(128)} %residual_hbm.1), custom_call_target="tpu_custom_call" | custom-call | tf_op jit(solution)/shard_map/pallas_call | solution.py:703
  33.2 0.8 %broadcast_multiply_fusion = f32[8,8,16,128]{3,2,1,0:T(8,128)} fusion(f32[8,8,16,128]{3,2,1,0:T(8,128)S(1)} %shard_map.46), kind=kLoop, calls=%fused_computation | loop fusion | flops 131072 | bytes 1048576 | tf_op jit(solution)/shard_map/mul | solution.py:729

commit v10 on v9

--- a/solution.py
+++ b/solution.py
@@ -138,7 +138,7 @@
         return pltpu.roll(a, 1, 0)
 
     def cells(by, bz):
-        return 0.5 * (by + y_ahead(by)), 0.5 * (bz + z_ahead(bz))
+        return by + y_ahead(by), bz + z_ahead(bz)
 
     def radial_edges(prev, cur, prev_drift, cur_drift):
         sum_x = prev[1] + cur[1]
@@ -181,11 +181,11 @@
             advs.append(viscous * lap - (half_x * dx + half_w * dy + half_z * dz))
 
         sum_bx = bx + nxt[5]
-        cx = 0.5 * sum_bx
-        cur_x = 0.5 * ((y_ahead(cz) - y_behind(cz)) - (z_ahead(cy) - z_behind(cy)))
-        cur_y = 0.5 * ((z_ahead(cx) - z_behind(cx)) - (cz_next - cz_prev))
-        cur_z = 0.5 * ((cy_next - cy_prev) - (y_ahead(cx) - y_behind(cx)))
-        inverse = jnp.exp(-log_rho)
+        cx = sum_bx
+        cur_x = (y_ahead(cz) - y_behind(cz)) - (z_ahead(cy) - z_behind(cy))
+        cur_y = (z_ahead(cx) - z_behind(cx)) - (cz_next - cz_prev)
+        cur_z = (cy_next - cy_prev) - (y_ahead(cx) - y_behind(cx))
+        inverse = 0.125 * jnp.exp(-log_rho)
         force_x = inverse * (cur_y * cz - cur_z * cy)
         force_y = inverse * (cur_z * cx - cur_x * cz)
         force_z = inverse * (cur_x * cy - cur_y * cx)
@@ -196,7 +196,7 @@
             advs[1] - (0.5 * sound_sq) * pairs[0] + force_x + (2.0 * rotation) * vy,
             advs[2] - (0.5 * sound_sq) * pairs[1] + force_y - ((2.0 - shear_rate) * rotation) * vx,
             advs[3] - (0.5 * sound_sq) * pairs[2] + force_z,
-            advs[4] + resist * inverse * (cur_x * cur_x + cur_y * cur_y + cur_z * cur_z),
+            advs[4] + (0.5 * resist) * inverse * (cur_x * cur_x + cur_y * cur_y + cur_z * cur_z),
         ]
 
         w_y, z_y = w + y_behind(w), vz + y_behind(vz)
@@ -537,8 +537,8 @@
         base = WINDOW * (row - i * kept)
         for f in range(fields):
             sides = windows_ref[i, f]
-            low = pltpu.roll(sides, 2 * cols - base - 8, 1)
-            high = pltpu.roll(sides, 2 * cols - base - 4, 1)
+            low = pltpu.roll(sides, cols - base - 8, 1)
+            high = pltpu.roll(sides, cols - base - 4, 1)
             total = moved_ref[f, row] + (cur[f] + time_step * rates[f])
             middle = jnp.where(lane >= cols - 2, high, total)
             out_ref[f, :, row - DEPTH, :] = jnp.where(lane < 2, low, middle)

time: 34.2 us -> 34.1 us (level)
  no operation moved by 1% of the time
where the time goes in v10:
time: 34.1 us; the launch traced here: 34 us
  Pallas kernels  32.5 us (95%)
  other arithmetic  0.84 us (2%)
  between operations  0.66 us (2%)
    pallas_call x1, Pallas kernels, spread(): pl.pallas_call(functools.partial(spread_kernel, groups, radial), out_shap...  32.5 us
    mul x1, other arithmetic, spread(): return 0.5 * out  0.84 us

profile of v10, /device:TPU:0, one launch (start us, length us, event | category | flops | bytes accessed | tf_op | source)
XLA Modules:
  0.0 34.0 jit_solution(292756945998552262)
XLA Ops:
  0.7 32.5 %shard_map.46 = f32[8,8,16,128]{3,2,1,0:T(8,128)S(1)} custom-call(f32[8,8,16,128]{3,2,1,0:T(8,128)} %state_ref.1, s32[16]{0:T(128)} %shift_hbm.1, s32[1]{0:T(128)S(6)} %copy.5.offset_hbm, f32[64]{0:T(128)} %residual_hbm.1), custom_call_target="tpu_custom_call" | custom-call | tf_op jit(solution)/shard_map/pallas_call | solution.py:703
  33.1 0.8 %broadcast_multiply_fusion = f32[8,8,16,128]{3,2,1,0:T(8,128)} fusion(f32[8,8,16,128]{3,2,1,0:T(8,128)S(1)} %shard_map.46), kind=kLoop, calls=%fused_computation | loop fusion | flops 131072 | bytes 1048576 | tf_op jit(solution)/shard_map/mul | solution.py:729

commit v11 on v9

--- a/solution.py
+++ b/solution.py
@@ -374,7 +374,7 @@
         return pl.ds(q * quarter, quarter)
 
     for pair in ((0, 3), (1, 2)):
-        for other in others:
+        for other in [others[k - 1] for k in (2, 3, 4, 5, 6, 7, 1)]:
             for q in pair:
                 remote(
                     state_ref.at[other[1], :, quarter_rows(q)], taken[q].at[gy], other, out_sent, q

time: 34.2 us -> 34.1 us (level)
  no operation moved by 1% of the time
where the time goes in v11:
time: 34.1 us; the launch traced here: 34 us
  Pallas kernels  32.5 us (95%)
  other arithmetic  0.84 us (2%)
  between operations  0.66 us (2%)
    pallas_call x1, Pallas kernels, spread(): pl.pallas_call(functools.partial(spread_kernel, groups, radial), out_shap...  32.5 us
    mul x1, other arithmetic, spread(): return 0.5 * out  0.84 us

profile of v11, /device:TPU:0, one launch (start us, length us, event | category | flops | bytes accessed | tf_op | source)
XLA Modules:
  0.0 34.0 jit_solution(17996288620424193683)
XLA Ops:
  0.7 32.5 %shard_map.46 = f32[8,8,16,128]{3,2,1,0:T(8,128)S(1)} custom-call(f32[8,8,16,128]{3,2,1,0:T(8,128)} %state_ref.1, s32[16]{0:T(128)} %shift_hbm.1, s32[1]{0:T(128)S(6)} %copy.5.offset_hbm, f32[64]{0:T(128)} %residual_hbm.1), custom_call_target="tpu_custom_call" | custom-call | tf_op jit(solution)/shard_map/pallas_call | solution.py:703
  33.1 0.8 %broadcast_multiply_fusion = f32[8,8,16,128]{3,2,1,0:T(8,128)} fusion(f32[8,8,16,128]{3,2,1,0:T(8,128)S(1)} %shard_map.46), kind=kLoop, calls=%fused_computation | loop fusion | flops 131072 | bytes 1048576 | tf_op jit(solution)/shard_map/mul | solution.py:729
